TPU v7x, 256 devices: a whole 4x4x8 slice. The times are simulated.
256 devices in a mesh: row: 8 (over x, core), col: 32 (over z, y).
Axes of the slice: x: 4, y: 4, z: 8, core: 2. Of those that a mesh axis runs over, the one named last changes fastest.
Arguments:
- momentum: float32 [5120, 27648], P('row', 'col'), may hold values from -130 to 130, as said below
- activations: bfloat16 [2048, 5120], P(None, 'row'), may hold values from -6 to 6
- out_grads: bfloat16 [2048, 27648], P(None, 'col'), may hold values from -0.125 to 0.125
- basis: float32 [27648, 256], P('col'), may hold values from -6 to 6
Outputs:
- new_momentum: float32 [5120, 27648], P('row', 'col')
- left_basis: float32 [5120, 256], P('row')
- new_basis: float32 [27648, 256], P('col')
Inputs may be any that keep to these rules, and one draw needn't show every extreme that they name: `momentum`: Real-valued entries of order one with varying row and column scales.
All inputs are finite; a program needn't handle non-finite values.
Results may differ from a plain program's by a relative error of at most 0.0003.
Values sent between devices are 32-bit elements; how exact they have to be, the bound alone decides.
A program may use at most 128 MiB of HBM per device.

v0:
```python
import math

import jax
import jax.numpy as jnp
from jax import lax
from jax.sharding import PartitionSpec as P

D = 5120
F = 27648


EPS = 1e-06
HIGH = lax.Precision.HIGHEST


def filled_up(lines, devices):
    spare = -lines.shape[0] % devices
    if not spare:
        return lines
    return jnp.concatenate([lines, jnp.zeros((spare, *lines.shape[1:]), lines.dtype)])


def joined_along(pieces, dim):
    shape = list(pieces.shape[1:])
    shape[dim] *= pieces.shape[0]
    return jnp.moveaxis(pieces, 0, dim).reshape(shape)


def from_everyone(x, axis):
    devices = lax.axis_size(axis)
    return lax.all_to_all(jnp.broadcast_to(x[None], (devices, *x.shape)), axis, 0, 0, tiled=True)


def gather_directly(x, axis, dim):
    return joined_along(from_everyone(x, axis), dim)


def in_blocks(x, dim, devices):
    shape = x.shape
    pieces = x.reshape(*shape[:dim], devices, shape[dim] // devices, *shape[dim + 1 :])
    return jnp.moveaxis(pieces, dim, 0)


def sent_and_summed(x, axis, dim):
    devices = lax.axis_size(axis)
    pieces = lax.all_to_all(in_blocks(x, dim, devices), axis, 0, 0, tiled=True)
    return jnp.sum(pieces, axis=0)


def sum_by_parts(x, axes):
    lines = x.reshape(-1, x.shape[-1])
    padded = filled_up(lines, lax.axis_size(axes))
    whole = gather_directly(sent_and_summed(padded, axes, 0), axes, 0)
    return lax.slice_in_dim(whole, 0, len(lines)).reshape(x.shape)


def of_everyone(x, axis):
    everything = from_everyone(x, axis)
    return jnp.sum(everything, axis=0)


def total_of_pieces(x, axis):
    pieces = lax.all_gather(x, axis)
    return pieces.sum(axis=0)


def left_product(block, factor_rows):
    return lax.dot_general(
        block,
        factor_rows,
        (((0,), (0,)), ((), ())),
        precision=HIGH,
        preferred_element_type=jnp.float32,
    )


def invert_gram(gram_total):
    factor = jnp.linalg.cholesky(gram_total)
    identity = jnp.eye(factor.shape[0], dtype=jnp.float32)
    return jax.scipy.linalg.solve_triangular(factor, identity, lower=True).T


def shards(momentum, activations, out_grads, basis):
    gradient = lax.dot_general(
        activations, out_grads, (((0,), (0,)), ((), ())), preferred_element_type=jnp.float32
    )
    merged = momentum + gradient
    block_rows = sum_by_parts(jnp.dot(merged, basis, precision=HIGH), "col")
    gram_part = jnp.dot(block_rows.T, block_rows, precision=HIGH)
    gram_total = of_everyone(gram_part, "row")
    inverse_t = invert_gram(gram_total)
    ortho = jnp.dot(block_rows, inverse_t, precision=HIGH)
    coeff_part = left_product(merged, block_rows)
    coeffs = total_of_pieces(coeff_part, "row")
    coeffs = jnp.dot(coeffs, inverse_t, precision=HIGH)
    squares = jnp.sum(coeffs * coeffs, axis=0)
    sq_total = of_everyone(squares, "col")
    new_momentum = merged - 0.5 * jnp.dot(ortho, coeffs.T, precision=HIGH)
    inv_norm = lax.rsqrt(sq_total / F + EPS)
    new_basis = coeffs * inv_norm[None, :]
    left_basis = ortho * jnp.float32(math.sqrt(D))
    return (new_momentum, left_basis, new_basis)


def solution(mesh):
    return jax.shard_map(
        shards,
        mesh=mesh,
        in_specs=(P("row", "col"), P(None, "row"), P(None, "col"), P("col", None)),
        out_specs=(P("row", "col"), P("row", None), P("col", None)),
        check_vma=False,
    )
```

profile of v0, /device:TPU:1, one launch (start us, length us, event | category | flops | bytes accessed | tf_op | source)
XLA Modules:
  0.0 274.4 jit_solution(8928861521625573885)
XLA Ops:
  7.2 1.9 copy-done
  9.2 5.5 %convolution_add_fusion = f32[640,864]{0,1:T(8,128)S(1)} fusion(f32[640,864]{0,1:T(8,128)} %param.4, bf16[2048,864]{0,1:T(8,128)(2,1)S(1)} %copy-done, bf16[2048,640]{1,0:T(8,128)(2,1)} %param.5), kind=kOutput, calls=%fused_computation.3 | convolution fusion | flops 2265477120 | bytes 10584064 | tf_op jit(solution)/shard_map/dot_general | solution.py:84
  14.6 1.3 copy-done.1
  16.0 4.7 %fusion.13 = f32[640,256]{1,0:T(8,128)} fusion(f32[640,864]{0,1:T(8,128)S(1)} %convolution_add_fusion, f32[864,256]{1,0:T(8,128)S(1)} %copy-done.4), kind=kOutput, calls=%fused_computation.41 | convolution fusion | flops 1698693120 | bytes 3751936 | tf_op jit(solution)/shard_map/dot_general | solution.py:88
  20.7 2.0 reshape.44
  22.8 33.2 %all_to_all.21 = f32[32,20,256]{2,1,0:T(8,128)} all-to-all(f32[32,20,256]{2,1,0:T(8,128)} %reshape.44), channel_id=1, replica_groups=mesh['row'=8,'col'=32] {'col'}, dimensions={0} | all-to-all | bytes 1310720 | tf_op jit(solution)/shard_map/all_to_all | solution.py:46
  56.0 1.8 reduce_sum.45
  57.8 0.8 broadcast_in_dim.7
  58.5 25.5 %all_to_all.22 = f32[32,20,256]{2,1,0:T(8,128)} all-to-all(f32[32,20,256]{2,1,0:T(8,128)S(1)} %broadcast_in_dim.7), channel_id=1, replica_groups=mesh['row'=8,'col'=32] {'col'}, dimensions={0} | all-to-all | bytes 1310720 | tf_op jit(solution)/shard_map/all_to_all | solution.py:31
  84.0 2.0 reshape.45
  86.0 4.9 %fusion.14 = f32[864,256]{1,0:T(8,128)} fusion(f32[640,864]{0,1:T(8,128)} %copy-done.1, f32[640,256]{1,0:T(8,128)} %reshape.45), kind=kOutput, calls=%fused_computation.42 | convolution fusion | flops 1698693120 | bytes 3751936 | tf_op jit(solution)/shard_map/dot_general | solution.py:68
  91.0 2.8 %convolution_bitcast_fusion = f32[256,256]{1,0:T(8,128)S(1)} fusion(f32[32,20,256]{2,1,0:T(8,128)} %all_to_all.22), kind=kOutput, calls=%fused_computation.4 | convolution fusion | flops 503316480 | bytes 917504 | tf_op jit(solution)/shard_map/dot_general | solution.py:89
  93.8 1.5 broadcast_in_dim.8
  95.3 8.5 %all-to-all-start.2 = ((f32[8,256,256]{2,1,0:T(8,128)}), f32[8,256,256]{2,1,0:T(8,128)}, u32[]{:S(2)}, u32[]{:S(2)}) async-start(f32[8,256,256]{2,1,0:T(8,128)} %broadcast_in_dim.8), calls=%async_computation.2 | async-start | bytes 4194304 | tf_op jit(solution)/shard_map/all_to_all | solution.py:31
  103.7 0.6 iota_compare_fusion
  104.4 48.0 %all-to-all-done.2 = f32[8,256,256]{2,1,0:T(8,128)} async-done(((f32[8,256,256]{2,1,0:T(8,128)}), f32[8,256,256]{2,1,0:T(8,128)}, u32[]{:S(2)}, u32[]{:S(2)}) %all-to-all-start.2) | async-done | bytes 2097184 | tf_op jit(solution)/shard_map/all_to_all | solution.py:31
  152.4 2.5 reduce_sum.46
  154.9 1.8 copy.14
  156.7 1.1 fusion
  157.8 0.7 copy-done.5
  158.5 0.6 cholesky.118
  159.1 13.2 %cholesky.50 = f32[128,128]{1,0:T(8,128)} custom-call(f32[128,128]{1,0:T(8,128)} %cholesky.118), custom_call_target="Cholesky" | custom-call | tf_op jit(solution)/shard_map/jit(cholesky)/cholesky | solution.py:78
  172.3 1.6 cholesky.113
  173.8 1.5 select_reduce_fusion.1
  175.3 11.3 %custom-call.15 = f32[1,128,128]{1,2,0:T(8,128)} custom-call(f32[1,128,128]{2,1,0:T(8,128)} %get-tuple-element.24), custom_call_target="InvertDiagBlocksLowerTriangular" | custom-call | tf_op jit(solution)/shard_map/jit(cholesky)/cholesky | solution.py:78
  186.6 1.7 constant_dynamic-update-slice_fusion.1
  188.3 1.7 convolution_subtract_fusion.1
  190.0 13.2 %cholesky.105 = f32[128,128]{1,0:T(8,128)} custom-call(f32[128,128]{1,0:T(8,128)} %convolution_subtract_fusion.1), custom_call_target="Cholesky" | custom-call | tf_op jit(solution)/shard_map/jit(cholesky)/cholesky | solution.py:78
  203.2 1.5 select_reduce_fusion
  204.6 0.7 compare_reduce_fusion
  206.6 1.7 select_select_fusion
  208.3 6.9 %while.1 = (s32[]{:T(128)}, f32[256,256]{1,0:T(8,128)}, s32[2,2]{1,0:T(2,128)S(1)}, f32[2,128,128]{2,1,0:T(8,128)}, s32[]{:T(128)}) while((s32[]{:T(128)}, f32[256,256]{1,0:T(8,128)}, s32[2,2]{1,0:T(2,128)S(1)}, f32[2,128,128]{2,1,0:T(8,128)}, s32[]{:T(128)}) %tuple.29), condition=%wide.while_cond, body=%wide.while_body.sunk | while | flops 2 | bytes 132705 | solution.py:80
  208.9 2.9 %bitcast_dynamic-update-slice_fusion.2 = f32[2,128,128]{2,1,0:T(8,128)} fusion(f32[2,128,128]{2,1,0:T(8,128)} %get-tuple-element.70, s32[]{:T(128)} %get-tuple-element.67, f32[256,256]{1,0:T(8,128)} %get-tuple-element.73, s32[]{:T(128)} %bitcast.44, s32[]{:T(128)} %bitcast.45), kind=kLoop, calls=%fused_computation.clone.1 | loop fusion | bytes 132608 | tf_op jit(solution)/shard_map/jit(_solve_triangular)/triangular_solve
  212.4 2.8 %bitcast_dynamic-update-slice_fusion.2 = f32[2,128,128]{2,1,0:T(8,128)} fusion(f32[2,128,128]{2,1,0:T(8,128)} %get-tuple-element.70, s32[]{:T(128)} %get-tuple-element.67, f32[256,256]{1,0:T(8,128)} %get-tuple-element.73, s32[]{:T(128)} %bitcast.44, s32[]{:T(128)} %bitcast.45), kind=kLoop, calls=%fused_computation.clone.1 | loop fusion | bytes 132608 | tf_op jit(solution)/shard_map/jit(_solve_triangular)/triangular_solve
  215.2 21.1 %custom-call.16 = f32[2,128,128]{1,2,0:T(8,128)} custom-call(f32[2,128,128]{2,1,0:T(8,128)} %get-tuple-element.10), custom_call_target="InvertDiagBlocksLowerTriangular" | custom-call | tf_op jit(solution)/shard_map/jit(_solve_triangular)/triangular_solve | solution.py:80
  236.3 1.1 fusion.3
  237.4 1.2 convolution_subtract_fusion
  238.6 1.1 fusion.6
  239.8 0.6 copy-done.3
  240.4 2.9 %broadcast_multiply_fusion.1 = (f32[640,256]{1,0:T(8,128)}, f32[640,256]{1,0:T(8,128)}) fusion(f32[640,256]{1,0:T(8,128)} %reshape.45, f32[128,256]{1,0:T(8,128)S(1)} %fusion.6, f32[128,256]{1,0:T(8,128)S(1)} %fusion.3), kind=kOutput, calls=%fused_computation.9 | convolution fusion | flops 503545856 | bytes 2228224 | tf_op jit(solution)/shard_map/dot_general | solution.py:92
  243.3 4.5 %reduce_sum.47 = f32[864,256]{1,0:T(8,128)} reduce(f32[8,864,256]{2,1,0:T(8,128)} %bitcast.46, f32[]{:T(128)} %constant.80.clone.1), dimensions={0}, to_apply=%region_6.7 | reduce | flops 1548288 | bytes 7962628 | tf_op jit(solution)/shard_map/reduce_sum | solution.py:64
  247.7 3.0 %multiply_reduce_fusion = (f32[256]{0:T(256)S(1)}, f32[864,256]{1,0:T(8,128)}) fusion(f32[864,256]{1,0:T(8,128)} %reduce_sum.47, f32[128,256]{1,0:T(8,128)} %copy-done.3, f32[128,256]{1,0:T(8,128)} %copy-done.2), kind=kOutput, calls=%fused_computation.7 | convolution fusion | flops 679984896 | bytes 2032640 | tf_op jit(solution)/shard_map/dot_general | solution.py:95
  250.8 0.6 broadcast_in_dim.10
  251.4 4.6 %all-to-all-start.3 = ((f32[32,1,256]{2,1,0:T(1,128)}), f32[32,1,256]{2,1,0:T(1,128)}, u32[]{:S(2)}, u32[]{:S(2)}) async-start(f32[32,1,256]{2,1,0:T(1,128)} %broadcast_in_dim.10), calls=%async_computation.3 | async-start | bytes 65536 | tf_op jit(solution)/shard_map/all_to_all | solution.py:31
  256.0 5.8 %multiply_subtract_fusion = f32[640,864]{0,1:T(8,128)} fusion(f32[640,864]{0,1:T(8,128)} %copy-done.1, f32[640,256]{1,0:T(8,128)} %get-tuple-element.28, f32[864,256]{1,0:T(8,128)} %get-tuple-element.30), kind=kOutput, calls=%fused_computation.2 | convolution fusion | flops 1699799040 | bytes 5963776 | tf_op jit(solution)/shard_map/dot_general | solution.py:98
  261.8 2.8 %all-to-all-done.3 = f32[32,1,256]{2,1,0:T(1,128)} async-done(((f32[32,1,256]{2,1,0:T(1,128)}), f32[32,1,256]{2,1,0:T(1,128)}, u32[]{:S(2)}, u32[]{:S(2)}) %all-to-all-start.3) | async-done | bytes 32800 | tf_op jit(solution)/shard_map/all_to_all | solution.py:31
  264.6 0.8 reduce_sum.49
  265.4 2.1 broadcast_multiply_fusion
  (19 shorter events, 1.4 us)
Async XLA Ops:
  7.2 2.0 copy-start
  7.2 236.1 %all-gather.3.cloned.1.call-start = ((), (), s32[]{:S(2)}) async-start(), calls=%async_computation.4 | async-start | bytes 7962624 | tf_op jit(solution)/shard_map/all_gather | solution.py:63
  9.2 6.8 %copy-start.4 = (f32[864,256]{1,0:T(8,128)S(1)}, f32[864,256]{1,0:T(8,128)}, u32[]{:S(2)}) copy-start(f32[864,256]{1,0:T(8,128)} %param.7) | copy-start | bytes 2654212
  14.6 1.4 copy-start.1
  95.3 57.1 %all-to-all-start.2 = ((f32[8,256,256]{2,1,0:T(8,128)}), f32[8,256,256]{2,1,0:T(8,128)}, u32[]{:S(2)}, u32[]{:S(2)}) async-start(f32[8,256,256]{2,1,0:T(8,128)} %broadcast_in_dim.8), calls=%async_computation.2 | async-start | bytes 4194304 | tf_op jit(solution)/shard_map/all_to_all | solution.py:31
  157.8 0.7 copy-start.5
  237.4 2.3 copy-start.2
  239.8 0.6 copy-start.3
  251.4 13.2 %all-to-all-start.3 = ((f32[32,1,256]{2,1,0:T(1,128)}), f32[32,1,256]{2,1,0:T(1,128)}, u32[]{:S(2)}, u32[]{:S(2)}) async-start(f32[32,1,256]{2,1,0:T(1,128)} %broadcast_in_dim.10), calls=%async_computation.3 | async-start | bytes 65536 | tf_op jit(solution)/shard_map/all_to_all | solution.py:31
Sparse Core Ops, SparseCore 0:
  91.1 69.4 all-gather.2
where the time goes:
time: 276 us; the launch traced here: 274 us
  other arithmetic  77.4 us (28%)
  blocking collectives  58.7 us (21%)
  waiting for transfers between devices  50.8 us (18%)
  matrix products  36.4 us (13%)
  local copies, waits for them, and re-layouts  22.6 us (8%)
  between operations  15.4 us (6%)
  starting transfers between devices  13.1 us (5%)
    all_to_all x2, waiting for transfers between devices, from_everyone(): lax.all_to_all(jnp.broadcast_to(x[None], (devices, *x.shape)), axis, 0, 0...  50.8 us
    another operation x6, other arithmetic, invert_gram(): factor = jnp.linalg.cholesky(gram_total)  41.2 us
    all_to_all x1, blocking collectives, sent_and_summed(): pieces = lax.all_to_all(in_blocks(x, dim, devices), axis, 0, 0, tiled=True)  33.2 us
    all_to_all x1, blocking collectives, from_everyone(): lax.all_to_all(jnp.broadcast_to(x[None], (devices, *x.shape)), axis, 0, 0...  25.5 us
    another operation x3, other arithmetic, invert_gram(): return jax.scipy.linalg.solve_triangular(factor, identity, lower=True).T  22.8 us
    all_to_all x2, starting transfers between devices, from_everyone(): lax.all_to_all(jnp.broadcast_to(x[None], (devices, *x.shape)), axis, 0, 0...  13 us
    another operation x6, local copies, waits for them, and re-layouts  6.89 us
    dot_general x1, matrix products, shards(): new_momentum = merged - 0.5 * jnp.dot(ortho, coeffs.T, precision=HIGH)  5.82 us
  transfers between devices with their start and end apart: 3, of which 2 were waited for; matrix products, arithmetic and copies ran while one was open for 36% of the time, Pallas kernels for 0%

commit v1 on v0

v1 whole, which is shorter than its diff:
```python
import math

import jax
import jax.numpy as jnp
from jax import lax
from jax.experimental import pallas as pl
from jax.experimental.pallas import tpu as pltpu
from jax.sharding import PartitionSpec as P

D = 5120
F = 27648
EPS = 1e-06
HIGH = lax.Precision.HIGHEST
MESH = pl.DeviceIdType.MESH
F32 = jnp.float32
BF16 = jnp.bfloat16

XS, YS, ZS = 4, 4, 8
ROWS, COLS, RANK, TOKENS = 640, 864, 256, 2048
COLS_PAD = 896
STEP = 288
GROUPS = ((0, 2), (2, 2), (4, 1))


def mm(a, b, ca, cb):
    return lax.dot_general(a, b, (((ca,), (cb,)), ((), ())), precision=HIGH, preferred_element_type=F32)


def mm16(a, b, ca, cb):
    return lax.dot_general(a, b, (((ca,), (cb,)), ((), ())), preferred_element_type=F32)


def halves(x):
    hi = x.astype(BF16)
    return hi, (x - hi.astype(F32)).astype(BF16)


def mm3(a, b, ca, cb):
    return mm16(a[0], b[0], ca, cb) + (mm16(a[0], b[1], ca, cb) + mm16(a[1], b[0], ca, cb))


def lane_of(v, c):
    return jnp.broadcast_to(v[:, c:c + 1], v.shape)

def row_of(v, r):
    return jnp.broadcast_to(v[r:r + 1, :], v.shape)

def inverse_factor_64(block):
    r64 = lax.broadcasted_iota(jnp.int32, (64, 64), 0)
    c64 = lax.broadcasted_iota(jnp.int32, (64, 64), 1)
    eye = jnp.where(r64 == c64, 1.0, 0.0).astype(jnp.float32)
    wide = jnp.concatenate([block, eye], axis=1)
    t = [wide[8 * k:8 * k + 8] for k in range(8)]
    sub = lax.broadcasted_iota(jnp.int32, (8, 128), 0)
    out = []
    for k in range(8):
        cols = [lane_of(t[k], 8 * k + c) for c in range(8)]
        e = [[row_of(cols[c], r) if r >= c else None for c in range(8)] for r in range(8)]
        rows = [row_of(t[k], r) for r in range(8)]
        rs = [None] * 8
        l = [[None] * 8 for _ in range(8)]
        for c in range(8):
            rs[c] = lax.rsqrt(e[c][c])
            rows[c] = rows[c] * rs[c]
            for r in range(c + 1, 8):
                l[r][c] = e[r][c] * rs[c]
            for r in range(c + 1, 8):
                for m in range(c + 1, r + 1):
                    e[r][m] = e[r][m] - l[r][c] * l[m][c]
                rows[r] = rows[r] - l[r][c] * rows[c]
        u = rows[0]
        for c in range(1, 8):
            u = jnp.where(sub == c, rows[c], u)
        out.append(u)
        for j in range(k + 1, 8):
            s = [lane_of(t[j], 8 * k + c) for c in range(8)]
            for c in range(8):
                s[c] = s[c] * rs[c]
                for m in range(c + 1, 8):
                    s[m] = s[m] - s[c] * l[m][c]
                t[j] = t[j] - s[c] * rows[c]
    return jnp.concatenate(out, axis=0)[:, 64:]

def joined(w11, w21, w22):
    top = jnp.concatenate([w11, jnp.zeros_like(w11)], axis=1)
    return jnp.concatenate([top, jnp.concatenate([w21, w22], axis=1)], axis=0)

def inverse_factor_step(a11, a21, a22, smaller):
    w11 = smaller(a11)
    l21 = mm(a21, w11, 1, 1)
    s = a22 - mm(l21, l21, 1, 1)
    lw = mm(l21, w11, 1, 0)
    w22 = smaller(s)
    w21 = -mm(w22, lw, 1, 0)
    return w11, w21, w22

def inverse_factor_128(a):
    return joined(*inverse_factor_step(a[:64, :64], a[64:, :64], a[64:, 64:], inverse_factor_64))


def kernel(mom_hbm, act_hbm, grad_hbm, basis_hbm, newm_hbm, left_hbm, newb_hbm,
           grad, act, merged, basis, bt_hi, bt_lo, m_hi, m_lo,
           part, from_y, mine, from_z, full,
           gram, gram_pair, gram_x, gram_all,
           coef, coef_pair, coef_sum, coef_x, coef_all,
           right, r_hi, r_lo, left, sq_z, sq_y,
           send, recv, local):
    row, col = lax.axis_index("row"), lax.axis_index("col")
    x, core = row // 2, lax.rem(row, 2)
    z, y = col // YS, lax.rem(col, YS)

    def at_y(d):
        return (row, z * YS + lax.rem(y + d, YS))

    def at_z(d):
        return (row, lax.rem(z + d, ZS) * YS + y)

    def at_x(d):
        return (lax.rem(x + d, XS) * 2 + core, col)

    other = (x * 2 + 1 - core, col)

    loads = [
        pltpu.make_async_copy(act_hbm.at[:, pl.ds(128 * t, 128 * n)], act.at[:, pl.ds(128 * t, 128 * n)], local.at[i])
        for i, (t, n) in enumerate(GROUPS)
    ]
    grad_load = [
        pltpu.make_async_copy(grad_hbm.at[pl.ds(STEP * i, STEP)], grad.at[pl.ds(STEP * i, STEP)], local.at[3 + i])
        for i in range(3)
    ]
    mom_load = pltpu.make_async_copy(mom_hbm, merged, local.at[6])
    basis_load = pltpu.make_async_copy(basis_hbm, basis.at[pl.ds(0, COLS)], local.at[7])
    basis_load.start()
    loads[0].start()
    for c in grad_load:
        c.start()
    mom_load.start()
    loads[1].start()
    loads[2].start()

    barrier = pltpu.get_barrier_semaphore()
    peers = [at_y(d) for d in range(1, YS)] + [at_z(d) for d in range(1, ZS)] + [at_x(d) for d in range(1, XS)] + [other]
    for peer in peers:
        pl.semaphore_signal(barrier, inc=1, device_id=peer, device_id_type=MESH)

    count = [0]
    started = []

    def remote(src, dst, peer):
        n = count[0]
        count[0] += 1
        copy = pltpu.make_async_remote_copy(
            src_ref=src, dst_ref=dst, send_sem=send.at[n], recv_sem=recv.at[n], device_id=peer, device_id_type=MESH)
        copy.start()
        started.append(copy)
        return copy

    basis[COLS:, :] = jnp.zeros((COLS_PAD - COLS, RANK), F32)
    m_hi[COLS:, :] = jnp.zeros((COLS_PAD - COLS, ROWS), BF16)
    m_lo[COLS:, :] = jnp.zeros((COLS_PAD - COLS, ROWS), BF16)
    basis_load.wait()
    for i in range(COLS_PAD // 128):
        hi, lo = halves(basis[128 * i:128 * i + 128, :].T)
        bt_hi[:, 128 * i:128 * i + 128] = hi
        bt_lo[:, 128 * i:128 * i + 128] = lo

    def project(g):
        t, n = GROUPS[g]
        lanes = slice(128 * t, 128 * (t + n))
        loads[g].wait()
        if g == 0:
            for c in grad_load:
                c.wait()
            mom_load.wait()

        @pl.loop(0, COLS // STEP)
        def _(i):
            rows = pl.ds(pl.multiple_of(i * STEP, STEP), STEP)
            m = merged[rows, lanes] + mm16(grad[rows, :], act[:, lanes], 1, 0)
            merged[rows, lanes] = m
            hi, lo = halves(m)
            m_hi[rows, lanes] = hi
            m_lo[rows, lanes] = lo

        p = mm3((bt_hi[...], bt_lo[...]), (m_hi[:, lanes], m_lo[:, lanes]), 1, 0)
        for k in range(n):
            part[t + k] = p[:, 128 * k:128 * k + 128]

    def span(g):
        return pl.ds(*GROUPS[g])

    def mine_y(d):
        return pl.ds(pl.multiple_of(64 * lax.rem(y + d, YS), 64), 64)

    def mine_z(d):
        return pl.ds(pl.multiple_of(8 * lax.rem(z + d, ZS), 8), 8)

    own = pl.ds(pl.multiple_of(64 * y + 8 * z, 8), 8)

    def scatter_y(g):
        return [remote(part.at[span(g), mine_y(d)], from_y.at[d - 1, span(g)], at_y(d)) for d in range(1, YS)]

    def scatter_z(g, before):
        for c in before:
            c.wait_recv()
        t, n = GROUPS[g]
        for k in range(t, t + n):
            mine[k] = (part[k, mine_y(0), :] + from_y[0, k]) + (from_y[1, k] + from_y[2, k])
        return [remote(mine.at[span(g), mine_z(d)], from_z.at[d - 1, span(g)], at_z(d)) for d in range(1, ZS)]

    def gather_z(g, before):
        for c in before:
            c.wait_recv()
        t, n = GROUPS[g]
        for k in range(t, t + n):
            total = mine[k, mine_z(0), :]
            for d in range(ZS - 1):
                total = total + from_z[d, k]
            full[k, own, :] = total
        return [remote(full.at[span(g), own], full.at[span(g), own], at_z(d)) for d in range(1, ZS)]

    def gather_y(g, before):
        for c in before:
            c.wait_recv()
        return [remote(full.at[span(g), mine_y(0)], full.at[span(g), mine_y(0)], at_y(d)) for d in range(1, YS)]

    def whole(g):
        t, n = GROUPS[g]
        return jnp.concatenate([full[k] for k in range(t, t + n)], axis=1)

    def coefficients(g):
        t, n = GROUPS[g]
        lanes = slice(128 * t, 128 * (t + n))
        p = halves(whole(g))

        @pl.loop(0, COLS // STEP)
        def _(i):
            rows = pl.ds(pl.multiple_of(i * STEP, STEP), STEP)
            c = mm3((m_hi[rows, lanes], m_lo[rows, lanes]), p, 1, 1)
            for k in range(2):
                v = c[:, 128 * k:128 * k + 128]
                coef[k, rows, :] = v if g == 0 else coef[k, rows, :] + v

    project(0)
    pl.semaphore_wait(barrier, len(peers))
    a0 = scatter_y(0)
    project(1)
    a1 = scatter_y(1)
    b0 = scatter_z(0, a0)
    project(2)
    a2 = scatter_y(2)
    b1 = scatter_z(1, a1)
    c0 = gather_z(0, b0)
    b2 = scatter_z(2, a2)
    c1 = gather_z(1, b1)
    d0 = gather_y(0, c0)
    c2 = gather_z(2, b2)
    d1 = gather_y(1, c1)
    d2 = gather_y(2, c2)
    for c in d0:
        c.wait_recv()
    gr = mm(whole(0), whole(0), 1, 1)
    coefficients(0)
    for c in d1:
        c.wait_recv()
    gr = gr + mm(whole(1), whole(1), 1, 1)
    coefficients(1)
    for c in d2:
        c.wait_recv()
    gr = gr + mm(whole(2), whole(2), 1, 1)

    gram[0] = gr[:128, :128]
    gram[1] = gr[128:, :128]
    gram[2] = gr[128:, 128:]
    half = pl.ds(pl.multiple_of(64 * core, 64), 64)
    other_half = pl.ds(pl.multiple_of(64 * (1 - core), 64), 64)
    e0 = remote(gram.at[pl.ds(0, 1), other_half], gram_pair.at[pl.ds(0, 1)], other)
    e1 = remote(gram.at[pl.ds(1, 2), other_half], gram_pair.at[pl.ds(1, 2)], other)
    coefficients(2)
    h = remote(coef.at[1 - core], coef_pair, other)

    def gram_over_x(b, n, before):
        before.wait_recv()
        for k in range(b, b + n):
            gram_x[x, k] = gram[k, half, :] + gram_pair[k]
        return [remote(gram_x.at[x, pl.ds(b, n)], gram_x.at[x, pl.ds(b, n)], at_x(d)) for d in range(1, XS)]

    def gram_to_pair(b, n, before):
        for c in before:
            c.wait_recv()
        for k in range(b, b + n):
            gram_all[k, half, :] = (gram_x[0, k] + gram_x[1, k]) + (gram_x[2, k] + gram_x[3, k])
        return remote(gram_all.at[pl.ds(b, n), half], gram_all.at[pl.ds(b, n), half], other)

    f0 = gram_over_x(0, 1, e0)
    f1 = gram_over_x(1, 2, e1)

    def coef_rows(d):
        return pl.ds(pl.multiple_of(216 * lax.rem(x + d, XS), 216), 216)

    h.wait_recv()
    coef_sum[...] = coef[core] + coef_pair[...]
    r = [remote(coef_sum.at[coef_rows(d)], coef_x.at[d - 1], at_x(d)) for d in range(1, XS)]
    g0 = gram_to_pair(0, 1, f0)
    g0.wait_recv()
    a11 = gram_all[0]
    w11 = inverse_factor_64(a11[:64, :64])
    l21 = mm(a11[64:, :64], w11, 1, 1)
    s = a11[64:, 64:] - mm(l21, l21, 1, 1)
    lw = mm(l21, w11, 1, 0)
    g1 = gram_to_pair(1, 2, f1)
    w22 = inverse_factor_64(s)
    wa = joined(w11, -mm(w22, lw, 1, 0), w22)
    g1.wait_recv()
    a22 = gram_all[2]
    l21 = mm(gram_all[1], wa, 1, 1)
    s = a22 - mm(l21, l21, 1, 1)
    lwa = mm(l21, wa, 1, 0)
    for c in r:
        c.wait_recv()
    coef_all[core, coef_rows(0), :] = (coef_sum[coef_rows(0), :] + coef_x[0]) + (coef_x[1] + coef_x[2])
    q = [remote(coef_all.at[core, coef_rows(0)], coef_all.at[core, coef_rows(0)], at_x(d)) for d in range(1, XS)]
    w11 = inverse_factor_64(s[:64, :64])
    l21 = mm(s[64:, :64], w11, 1, 1)
    s2 = s[64:, 64:] - mm(l21, l21, 1, 1)
    lw = mm(l21, w11, 1, 0)
    for c in q:
        c.wait_recv()
    k0 = remote(coef_all.at[core], coef_all.at[core], other)
    w22 = inverse_factor_64(s2)
    wb = joined(w11, -mm(w22, lw, 1, 0), w22)
    w = joined(wa, -mm(wb, lwa, 1, 0), wb)

    k0.wait_recv()
    w_parts = halves(w)

    def finish(i, squares):
        rows = pl.ds(pl.multiple_of(i * STEP, STEP), STEP)
        c = jnp.concatenate([coef_all[0, rows, :], coef_all[1, rows, :]], axis=1)
        c = mm3(halves(c), w_parts, 1, 1)
        right[rows, :] = c
        hi, lo = halves(c)
        r_hi[rows, :] = hi
        r_lo[rows, :] = lo
        return squares + jnp.sum(c * c, axis=0, keepdims=True)

    squares = lax.fori_loop(0, COLS // STEP, finish, jnp.zeros((1, RANK), F32))
    sq_z[z] = squares
    n = [remote(sq_z.at[z], sq_z.at[z], at_z(d)) for d in range(1, ZS)]

    outs = []
    for g, (t, num) in enumerate(GROUPS):
        lanes = slice(128 * t, 128 * (t + num))
        ortho = mm3(w_parts, halves(whole(g)), 1, 0)
        left[lanes, :] = (ortho * F32(math.sqrt(D))).T
        o = halves(ortho)

        @pl.loop(0, COLS // STEP)
        def _(i):
            rows = pl.ds(pl.multiple_of(i * STEP, STEP), STEP)
            merged[rows, lanes] = merged[rows, lanes] - 0.5 * mm3((r_hi[rows, :], r_lo[rows, :]), o, 1, 0)

        if g == 1:
            for c in n:
                c.wait_recv()
            total = sq_z[0]
            for k in range(1, ZS):
                total = total + sq_z[k]
            sq_y[y] = total
            v = [remote(sq_y.at[y], sq_y.at[y], at_y(d)) for d in range(1, YS)]
        out = pltpu.make_async_copy(merged.at[:, lanes], newm_hbm.at[:, lanes], local.at[8 + g])
        out.start()
        outs.append(out)
    out = pltpu.make_async_copy(left, left_hbm, local.at[11])
    out.start()
    outs.append(out)
    for c in v:
        c.wait_recv()
    total = (sq_y[0] + sq_y[1]) + (sq_y[2] + sq_y[3])
    inv = lax.rsqrt(total / F + EPS)
    right[...] = right[...] * inv
    out = pltpu.make_async_copy(right, newb_hbm, local.at[12])
    out.start()
    outs.append(out)
    for c in started:
        c.wait_send()
    for out in outs:
        out.wait()


COPIES = 3 * 20 + 10 + 8 + 10


def shards(momentum, activations, out_grads, basis):
    any_ = pl.BlockSpec(memory_space=pl.ANY)
    new_t, left, right = pl.pallas_call(
        kernel,
        out_shape=(
            jax.ShapeDtypeStruct((COLS, ROWS), F32),
            jax.ShapeDtypeStruct((ROWS, RANK), F32),
            jax.ShapeDtypeStruct((COLS, RANK), F32),
        ),
        in_specs=[any_] * 4,
        out_specs=[any_] * 3,
        scratch_shapes=[
            pltpu.VMEM((COLS, TOKENS), BF16),
            pltpu.VMEM((TOKENS, ROWS), BF16),
            pltpu.VMEM((COLS, ROWS), F32),
            pltpu.VMEM((COLS_PAD, RANK), F32),
            pltpu.VMEM((RANK, COLS_PAD), BF16),
            pltpu.VMEM((RANK, COLS_PAD), BF16),
            pltpu.VMEM((COLS_PAD, ROWS), BF16),
            pltpu.VMEM((COLS_PAD, ROWS), BF16),
            pltpu.VMEM((5, RANK, 128), F32),
            pltpu.VMEM((YS - 1, 5, 64, 128), F32),
            pltpu.VMEM((5, 64, 128), F32),
            pltpu.VMEM((ZS - 1, 5, 8, 128), F32),
            pltpu.VMEM((5, RANK, 128), F32),
            pltpu.VMEM((3, 128, 128), F32),
            pltpu.VMEM((3, 64, 128), F32),
            pltpu.VMEM((XS, 3, 64, 128), F32),
            pltpu.VMEM((3, 128, 128), F32),
            pltpu.VMEM((2, COLS, 128), F32),
            pltpu.VMEM((COLS, 128), F32),
            pltpu.VMEM((COLS, 128), F32),
            pltpu.VMEM((XS - 1, 216, 128), F32),
            pltpu.VMEM((2, COLS, 128), F32),
            pltpu.VMEM((COLS, RANK), F32),
            pltpu.VMEM((COLS, RANK), BF16),
            pltpu.VMEM((COLS, RANK), BF16),
            pltpu.VMEM((ROWS, RANK), F32),
            pltpu.VMEM((ZS, 1, RANK), F32),
            pltpu.VMEM((YS, 1, RANK), F32),
            pltpu.SemaphoreType.DMA((COPIES,)),
            pltpu.SemaphoreType.DMA((COPIES,)),
            pltpu.SemaphoreType.DMA((13,)),
        ],
        compiler_params=pltpu.CompilerParams(
            collective_id=0, has_side_effects=True, vmem_limit_bytes=48 * 1024 * 1024),
    )(momentum.T, activations, out_grads.T, basis)
    return new_t.T, left, right


def solution(mesh):
    return jax.shard_map(
        shards,
        mesh=mesh,
        in_specs=(P("row", "col"), P(None, "row"), P(None, "col"), P("col", None)),
        out_specs=(P("row", "col"), P("row", None), P("col", None)),
        check_vma=False,
    )
```

time: 276 us -> 78.7 us (0.29)
  other arithmetic: 77.4 us -> 0 us
  Pallas kernels: 0 us -> 73.7 us
  blocking collectives: 58.7 us -> 0 us
  waiting for transfers between devices: 50.8 us -> 0 us
  matrix products: 36.4 us -> 0 us
  local copies, waits for them, and re-layouts: 22.6 us -> 4.27 us
  between operations: 15.4 us -> 0.65 us
  starting transfers between devices: 13.1 us -> 0 us
    pallas_call x0 -> x1, Pallas kernels: none -> 73.7 us  [shards(): pl.pallas_call(kernel, out_shape=(jax.ShapeDtypeStruct((COLS, ROWS), F32)...]
    another operation x9 -> x0, other arithmetic: 64 us -> none  [the longest x6 41.2 us: invert_gram(): factor = jnp.linalg.cholesky(gram_total)]
    all_to_all x2 -> x0, blocking collectives: 58.7 us -> none  [the longest x1 33.2 us: sent_and_summed(): pieces = lax.all_to_all(in_blocks(x, dim, devices), axis, 0, 0, tiled=True)]
    all_to_all x2 -> x0, waiting for transfers between devices: 50.8 us -> none  [from_everyone(): lax.all_to_all(jnp.broadcast_to(x[None], (devices, *x.shape)), axis, 0, 0...]
    dot_general x7 -> x0, matrix products: 29.6 us -> none  [the longest x1 5.82 us: shards(): new_momentum = merged - 0.5 * jnp.dot(ortho, coeffs.T, precision=HIGH)]
    all_to_all x2 -> x0, starting transfers between devices: 13 us -> none  [from_everyone(): lax.all_to_all(jnp.broadcast_to(x[None], (devices, *x.shape)), axis, 0, 0...]
    reduce_sum x4 -> x0, other arithmetic: 9.55 us -> none  [the longest x1 4.49 us: total_of_pieces(): return pieces.sum(axis=0)]
    another operation x9 -> x0, local copies, waits for them, and re-layouts: 9.15 us -> none
  transfers between devices with their start and end apart: 3 -> 0, of which waited for: 2 -> 0; matrix products, arithmetic and copies ran while one was open for 36% -> 0% of each run, Pallas kernels for 0% -> 0%
where the time goes in v1:
time: 78.7 us; the launch traced here: 78.6 us
  Pallas kernels  73.7 us (94%)
  local copies, waits for them, and re-layouts  4.27 us (5%)
    pallas_call x1, Pallas kernels, shards(): pl.pallas_call(kernel, out_shape=(jax.ShapeDtypeStruct((COLS, ROWS), F32)...  73.7 us
    unnamed x5, local copies, waits for them, and re-layouts  4.27 us

profile of v1, /device:TPU:1, one launch (start us, length us, event | category | flops | bytes accessed | tf_op | source)
XLA Modules:
  0.0 78.6 jit_solution(15926281916310494634)
XLA Ops:
  0.6 0.0 copy-start
  0.6 1.2 %copy-done = f32[864,256]{1,0:T(8,128)S(1)} copy-done((f32[864,256]{1,0:T(8,128)S(1)}, f32[864,256]{1,0:T(8,128)}, u32[]{:S(2)}) %copy-start) | copy-done | bytes 884760
  1.8 73.7 %shard_map.67 = (f32[864,640]{1,0:T(8,128)S(1)}, f32[640,256]{1,0:T(8,128)S(1)}, f32[864,256]{1,0:T(8,128)S(1)}) custom-call(f32[864,640]{1,0:T(8,128)} %bitcast.5, bf16[2048,640]{1,0:T(8,128)(2,1)} %act_hbm.1, bf16[864,2048]{1,0:T(8,128)(2,1)} %bitcast.4, f32[864,256]{1,0:T(8,128)S(1)} %copy-done), custom_call_target="tpu_custom_call" | custom-call | tf_op jit(solution)/shard_map/pallas_call | solution.py:396
  75.5 1.4 %copy.10 = f32[640,864]{0,1:T(8,128)} copy(f32[640,864]{0,1:T(8,128)S(1)} %bitcast.3) | data formatting | bytes 4423680
  76.8 0.8 %copy.11 = f32[640,256]{1,0:T(8,128)} copy(f32[640,256]{1,0:T(8,128)S(1)} %get-tuple-element.13) | data formatting | bytes 1310720
  77.7 0.9 %copy.12 = f32[864,256]{1,0:T(8,128)} copy(f32[864,256]{1,0:T(8,128)S(1)} %get-tuple-element.14) | data formatting | bytes 1769472
Async XLA Ops:
  0.6 1.2 %copy-start = (f32[864,256]{1,0:T(8,128)S(1)}, f32[864,256]{1,0:T(8,128)}, u32[]{:S(2)}) copy-start(f32[864,256]{1,0:T(8,128)} %basis_hbm.1) | copy-start | bytes 2654212

commit v2 on v1

--- a/solution.py
+++ b/solution.py
@@ -20,6 +20,7 @@
 COLS_PAD = 896
 STEP = 288
 GROUPS = ((0, 2), (2, 2), (4, 1))
+FAR_Z = (4, 3, 5, 2, 6, 1, 7)
 
 
 def mm(a, b, ca, cb):
@@ -98,12 +99,12 @@
     return joined(*inverse_factor_step(a[:64, :64], a[64:, :64], a[64:, 64:], inverse_factor_64))
 
 
-def kernel(mom_hbm, act_hbm, grad_hbm, basis_hbm, newm_hbm, left_hbm, newb_hbm,
+def kernel(mom_hbm, act_hbm, grad_hbm, basis_hbm, newm_hbm, left_hbm, newb_hbm, inv_hbm,
            grad, act, merged, basis, bt_hi, bt_lo, m_hi, m_lo,
-           part, from_y, mine, from_z, full,
+           part, pass_y, sum_y, from_y, mine, from_z, full,
            gram, gram_pair, gram_x, gram_all,
-           coef, coef_pair, coef_sum, coef_x, coef_all,
-           right, r_hi, r_lo, left, sq_z, sq_y,
+           coef, coef_pair, coef_sum, coef_mid, coef_x, coef_all,
+           right, r_hi, r_lo, left, sq_z, sq_y, inv,
            send, recv, local):
     row, col = lax.axis_index("row"), lax.axis_index("col")
     x, core = row // 2, lax.rem(row, 2)
@@ -128,13 +129,16 @@
         pltpu.make_async_copy(grad_hbm.at[pl.ds(STEP * i, STEP)], grad.at[pl.ds(STEP * i, STEP)], local.at[3 + i])
         for i in range(3)
     ]
-    mom_load = pltpu.make_async_copy(mom_hbm, merged, local.at[6])
+    mom_load = [
+        pltpu.make_async_copy(mom_hbm.at[pl.ds(STEP * i, STEP)], merged.at[pl.ds(STEP * i, STEP)], local.at[8 + i])
+        for i in range(3)
+    ]
     basis_load = pltpu.make_async_copy(basis_hbm, basis.at[pl.ds(0, COLS)], local.at[7])
     basis_load.start()
     loads[0].start()
-    for c in grad_load:
-        c.start()
-    mom_load.start()
+    for i in range(3):
+        grad_load[i].start()
+        mom_load[i].start()
     loads[1].start()
     loads[2].start()
 
@@ -168,13 +172,8 @@
         t, n = GROUPS[g]
         lanes = slice(128 * t, 128 * (t + n))
         loads[g].wait()
-        if g == 0:
-            for c in grad_load:
-                c.wait()
-            mom_load.wait()
-
-        @pl.loop(0, COLS // STEP)
-        def _(i):
+
+        def merge(i):
             rows = pl.ds(pl.multiple_of(i * STEP, STEP), STEP)
             m = merged[rows, lanes] + mm16(grad[rows, :], act[:, lanes], 1, 0)
             merged[rows, lanes] = m
@@ -182,6 +181,14 @@
             m_hi[rows, lanes] = hi
             m_lo[rows, lanes] = lo
 
+        if g == 0:
+            for i in range(COLS // STEP):
+                grad_load[i].wait()
+                mom_load[i].wait()
+                merge(i)
+        else:
+            pl.loop(0, COLS // STEP)(merge)
+
         p = mm3((bt_hi[...], bt_lo[...]), (m_hi[:, lanes], m_lo[:, lanes]), 1, 0)
         for k in range(n):
             part[t + k] = p[:, 128 * k:128 * k + 128]
@@ -197,16 +204,35 @@
 
     own = pl.ds(pl.multiple_of(64 * y + 8 * z, 8), 8)
 
+    def rows_of(d, at, n):
+        return pl.ds(pl.multiple_of(64 * lax.rem(y + d, YS) + at, 32), n)
+
     def scatter_y(g):
-        return [remote(part.at[span(g), mine_y(d)], from_y.at[d - 1, span(g)], at_y(d)) for d in range(1, YS)]
+        t = span(g)
+        return [
+            remote(part.at[t, rows_of(2, 0, 32)], pass_y.at[0, t], at_y(1)),
+            remote(part.at[t, rows_of(2, 32, 32)], pass_y.at[1, t], at_y(3)),
+            remote(part.at[t, rows_of(1, 32, 32)], from_y.at[0, t, pl.ds(32, 32)], at_y(1)),
+            remote(part.at[t, rows_of(3, 0, 32)], from_y.at[1, t, pl.ds(0, 32)], at_y(3)),
+        ]
+
+    def relay_y(g, before):
+        t, n = GROUPS[g]
+        after = before[2:]
+        for way, (d, at) in enumerate(((1, 0), (3, 32))):
+            before[way].wait_recv()
+            for k in range(t, t + n):
+                sum_y[way, k] = part[k, rows_of(d, at, 32), :] + pass_y[way, k]
+            after.append(remote(sum_y.at[way, span(g)], from_y.at[way, span(g), pl.ds(at, 32)], at_y(d)))
+        return after
 
     def scatter_z(g, before):
         for c in before:
             c.wait_recv()
         t, n = GROUPS[g]
         for k in range(t, t + n):
-            mine[k] = (part[k, mine_y(0), :] + from_y[0, k]) + (from_y[1, k] + from_y[2, k])
-        return [remote(mine.at[span(g), mine_z(d)], from_z.at[d - 1, span(g)], at_z(d)) for d in range(1, ZS)]
+            mine[k] = (part[k, mine_y(0), :] + from_y[0, k]) + from_y[1, k]
+        return [remote(mine.at[span(g), mine_z(d)], from_z.at[d - 1, span(g)], at_z(d)) for d in FAR_Z]
 
     def gather_z(g, before):
         for c in before:
@@ -217,12 +243,20 @@
             for d in range(ZS - 1):
                 total = total + from_z[d, k]
             full[k, own, :] = total
-        return [remote(full.at[span(g), own], full.at[span(g), own], at_z(d)) for d in range(1, ZS)]
+        return [remote(full.at[span(g), own], full.at[span(g), own], at_z(d)) for d in FAR_Z]
 
     def gather_y(g, before):
         for c in before:
             c.wait_recv()
-        return [remote(full.at[span(g), mine_y(0)], full.at[span(g), mine_y(0)], at_y(d)) for d in range(1, YS)]
+        return [remote(full.at[span(g), mine_y(0)], full.at[span(g), mine_y(0)], at_y(d)) for d in (1, 3)]
+
+    def pass_on_y(g, before):
+        after = []
+        for c, (source, to, at) in zip(before, ((3, 1, 0), (1, 3, 32))):
+            c.wait_recv()
+            block = full.at[span(g), rows_of(source, at, 32)]
+            after.append(remote(block, block, at_y(to)))
+        return after
 
     def whole(g):
         t, n = GROUPS[g]
@@ -246,20 +280,26 @@
     a0 = scatter_y(0)
     project(1)
     a1 = scatter_y(1)
-    b0 = scatter_z(0, a0)
+    a0 = relay_y(0, a0)
     project(2)
     a2 = scatter_y(2)
+    b0 = scatter_z(0, a0)
+    a1 = relay_y(1, a1)
+    a2 = relay_y(2, a2)
+    c0 = gather_z(0, b0)
     b1 = scatter_z(1, a1)
-    c0 = gather_z(0, b0)
     b2 = scatter_z(2, a2)
+    d0 = gather_y(0, c0)
     c1 = gather_z(1, b1)
-    d0 = gather_y(0, c0)
     c2 = gather_z(2, b2)
+    d0 = pass_on_y(0, d0)
     d1 = gather_y(1, c1)
     d2 = gather_y(2, c2)
+    d1 = pass_on_y(1, d1)
     for c in d0:
         c.wait_recv()
     gr = mm(whole(0), whole(0), 1, 1)
+    d2 = pass_on_y(2, d2)
     coefficients(0)
     for c in d1:
         c.wait_recv()
@@ -283,7 +323,15 @@
         before.wait_recv()
         for k in range(b, b + n):
             gram_x[x, k] = gram[k, half, :] + gram_pair[k]
-        return [remote(gram_x.at[x, pl.ds(b, n)], gram_x.at[x, pl.ds(b, n)], at_x(d)) for d in range(1, XS)]
+        return [remote(gram_x.at[x, pl.ds(b, n)], gram_x.at[x, pl.ds(b, n)], at_x(d)) for d in (1, 3)]
+
+    def gram_pass_on(b, n, before):
+        after = []
+        for c, (source, to, at) in zip(before, ((3, 1, 0), (1, 3, 32))):
+            c.wait_recv()
+            block = gram_x.at[lax.rem(x + source, XS), pl.ds(b, n), pl.ds(at, 32)]
+            after.append(remote(block, block, at_x(to)))
+        return after
 
     def gram_to_pair(b, n, before):
         for c in before:
@@ -295,13 +343,25 @@
     f0 = gram_over_x(0, 1, e0)
     f1 = gram_over_x(1, 2, e1)
 
-    def coef_rows(d):
-        return pl.ds(pl.multiple_of(216 * lax.rem(x + d, XS), 216), 216)
-
+    def coef_rows(d, at=0, n=216):
+        return pl.ds(pl.multiple_of(216 * lax.rem(x + d, XS) + at, 8), n)
+
+    def coef_to(d, block):
+        return remote(coef_all.at[core, block], coef_all.at[core, block], d)
+
+    f0 = gram_pass_on(0, 1, f0)
     h.wait_recv()
     coef_sum[...] = coef[core] + coef_pair[...]
-    r = [remote(coef_sum.at[coef_rows(d)], coef_x.at[d - 1], at_x(d)) for d in range(1, XS)]
+    r_pass = [
+        remote(coef_sum.at[coef_rows(2, 0, 112)], coef_x.at[2, pl.ds(0, 112)], at_x(1)),
+        remote(coef_sum.at[coef_rows(2, 112, 104)], coef_x.at[3, pl.ds(0, 104)], at_x(3)),
+    ]
+    r = [
+        remote(coef_sum.at[coef_rows(1, 112, 104)], coef_x.at[0, pl.ds(112, 104)], at_x(1)),
+        remote(coef_sum.at[coef_rows(3, 0, 112)], coef_x.at[1, pl.ds(0, 112)], at_x(3)),
+    ]
     g0 = gram_to_pair(0, 1, f0)
+    f1 = gram_pass_on(1, 2, f1)
     g0.wait_recv()
     a11 = gram_all[0]
     w11 = inverse_factor_64(a11[:64, :64])
@@ -309,6 +369,12 @@
     s = a11[64:, 64:] - mm(l21, l21, 1, 1)
     lw = mm(l21, w11, 1, 0)
     g1 = gram_to_pair(1, 2, f1)
+    r_pass[0].wait_recv()
+    coef_mid[0:112] = coef_sum[coef_rows(1, 0, 112), :] + coef_x[2, 0:112]
+    r.append(remote(coef_mid.at[pl.ds(0, 112)], coef_x.at[0, pl.ds(0, 112)], at_x(1)))
+    r_pass[1].wait_recv()
+    coef_mid[112:216] = coef_sum[coef_rows(3, 112, 104), :] + coef_x[3, 0:104]
+    r.append(remote(coef_mid.at[pl.ds(112, 104)], coef_x.at[1, pl.ds(112, 104)], at_x(3)))
     w22 = inverse_factor_64(s)
     wa = joined(w11, -mm(w22, lw, 1, 0), w22)
     g1.wait_recv()
@@ -318,20 +384,28 @@
     lwa = mm(l21, wa, 1, 0)
     for c in r:
         c.wait_recv()
-    coef_all[core, coef_rows(0), :] = (coef_sum[coef_rows(0), :] + coef_x[0]) + (coef_x[1] + coef_x[2])
-    q = [remote(coef_all.at[core, coef_rows(0)], coef_all.at[core, coef_rows(0)], at_x(d)) for d in range(1, XS)]
+    coef_all[core, coef_rows(0), :] = (coef_sum[coef_rows(0), :] + coef_x[0]) + coef_x[1]
+    q = [coef_to(at_x(1), coef_rows(0)), coef_to(at_x(3), coef_rows(0))]
+    k = [coef_to(other, coef_rows(0))]
     w11 = inverse_factor_64(s[:64, :64])
     l21 = mm(s[64:, :64], w11, 1, 1)
     s2 = s[64:, 64:] - mm(l21, l21, 1, 1)
     lw = mm(l21, w11, 1, 0)
-    for c in q:
-        c.wait_recv()
-    k0 = remote(coef_all.at[core], coef_all.at[core], other)
+    q[0].wait_recv()
+    q.append(coef_to(at_x(1), coef_rows(3, 0, 112)))
+    k.append(coef_to(other, coef_rows(3)))
+    q[1].wait_recv()
+    q.append(coef_to(at_x(3), coef_rows(1, 112, 104)))
+    k.append(coef_to(other, coef_rows(1)))
     w22 = inverse_factor_64(s2)
     wb = joined(w11, -mm(w22, lw, 1, 0), w22)
     w = joined(wa, -mm(wb, lwa, 1, 0), wb)
-
-    k0.wait_recv()
+    q[2].wait_recv()
+    q[3].wait_recv()
+    k.append(coef_to(other, coef_rows(2)))
+
+    for c in k:
+        c.wait_recv()
     w_parts = halves(w)
 
     def finish(i, squares):
@@ -368,18 +442,17 @@
                 total = total + sq_z[k]
             sq_y[y] = total
             v = [remote(sq_y.at[y], sq_y.at[y], at_y(d)) for d in range(1, YS)]
-        out = pltpu.make_async_copy(merged.at[:, lanes], newm_hbm.at[:, lanes], local.at[8 + g])
+        out = pltpu.make_async_copy(merged.at[:, lanes], newm_hbm.at[:, lanes], local.at[11 + g])
         out.start()
         outs.append(out)
-    out = pltpu.make_async_copy(left, left_hbm, local.at[11])
-    out.start()
-    outs.append(out)
+    for src, dst, i in ((left, left_hbm, 14), (right, newb_hbm, 15)):
+        out = pltpu.make_async_copy(src, dst, local.at[i])
+        out.start()
+        outs.append(out)
     for c in v:
         c.wait_recv()
-    total = (sq_y[0] + sq_y[1]) + (sq_y[2] + sq_y[3])
-    inv = lax.rsqrt(total / F + EPS)
-    right[...] = right[...] * inv
-    out = pltpu.make_async_copy(right, newb_hbm, local.at[12])
+    inv[...] = lax.rsqrt(((sq_y[0] + sq_y[1]) + (sq_y[2] + sq_y[3])) / F + EPS)
+    out = pltpu.make_async_copy(inv, inv_hbm, local.at[16])
     out.start()
     outs.append(out)
     for c in started:
@@ -388,20 +461,35 @@
         out.wait()
 
 
-COPIES = 3 * 20 + 10 + 8 + 10
+def write_out(new, left, right, inv, new_hbm, left_hbm, right_hbm, scaled, sems):
+    outs = [
+        pltpu.make_async_copy(new, new_hbm, sems.at[0]),
+        pltpu.make_async_copy(left, left_hbm, sems.at[1]),
+        pltpu.make_async_copy(scaled, right_hbm, sems.at[2]),
+    ]
+    outs[0].start()
+    outs[1].start()
+    scaled[...] = right[...] * inv[...]
+    outs[2].start()
+    for out in outs:
+        out.wait()
+
+
+COPIES = 3 * 24 + 12 + 15 + 10
 
 
 def shards(momentum, activations, out_grads, basis):
     any_ = pl.BlockSpec(memory_space=pl.ANY)
-    new_t, left, right = pl.pallas_call(
+    new_t, left, right, inv = pl.pallas_call(
         kernel,
         out_shape=(
             jax.ShapeDtypeStruct((COLS, ROWS), F32),
             jax.ShapeDtypeStruct((ROWS, RANK), F32),
             jax.ShapeDtypeStruct((COLS, RANK), F32),
+            jax.ShapeDtypeStruct((1, RANK), F32),
         ),
-        in_specs=[any_] * 4,
-        out_specs=[any_] * 3,
+        in_specs=[pl.BlockSpec(memory_space=pltpu.HBM)] * 4,
+        out_specs=[any_] * 4,
         scratch_shapes=[
             pltpu.VMEM((COLS, TOKENS), BF16),
             pltpu.VMEM((TOKENS, ROWS), BF16),
@@ -412,7 +500,9 @@
             pltpu.VMEM((COLS_PAD, ROWS), BF16),
             pltpu.VMEM((COLS_PAD, ROWS), BF16),
             pltpu.VMEM((5, RANK, 128), F32),
-            pltpu.VMEM((YS - 1, 5, 64, 128), F32),
+            pltpu.VMEM((2, 5, 32, 128), F32),
+            pltpu.VMEM((2, 5, 32, 128), F32),
+            pltpu.VMEM((2, 5, 64, 128), F32),
             pltpu.VMEM((5, 64, 128), F32),
             pltpu.VMEM((ZS - 1, 5, 8, 128), F32),
             pltpu.VMEM((5, RANK, 128), F32),
@@ -423,7 +513,8 @@
             pltpu.VMEM((2, COLS, 128), F32),
             pltpu.VMEM((COLS, 128), F32),
             pltpu.VMEM((COLS, 128), F32),
-            pltpu.VMEM((XS - 1, 216, 128), F32),
+            pltpu.VMEM((216, 128), F32),
+            pltpu.VMEM((4, 216, 128), F32),
             pltpu.VMEM((2, COLS, 128), F32),
             pltpu.VMEM((COLS, RANK), F32),
             pltpu.VMEM((COLS, RANK), BF16),
@@ -431,13 +522,27 @@
             pltpu.VMEM((ROWS, RANK), F32),
             pltpu.VMEM((ZS, 1, RANK), F32),
             pltpu.VMEM((YS, 1, RANK), F32),
+            pltpu.VMEM((1, RANK), F32),
             pltpu.SemaphoreType.DMA((COPIES,)),
             pltpu.SemaphoreType.DMA((COPIES,)),
-            pltpu.SemaphoreType.DMA((13,)),
+            pltpu.SemaphoreType.DMA((17,)),
         ],
         compiler_params=pltpu.CompilerParams(
             collective_id=0, has_side_effects=True, vmem_limit_bytes=48 * 1024 * 1024),
     )(momentum.T, activations, out_grads.T, basis)
+    vmem = pl.BlockSpec(memory_space=pltpu.VMEM)
+    new_t, left, right = pl.pallas_call(
+        write_out,
+        out_shape=(
+            jax.ShapeDtypeStruct((COLS, ROWS), F32),
+            jax.ShapeDtypeStruct((ROWS, RANK), F32),
+            jax.ShapeDtypeStruct((COLS, RANK), F32),
+        ),
+        in_specs=[any_, any_, vmem, vmem],
+        out_specs=[any_] * 3,
+        scratch_shapes=[pltpu.VMEM((COLS, RANK), F32), pltpu.SemaphoreType.DMA((3,))],
+        compiler_params=pltpu.CompilerParams(vmem_limit_bytes=8 * 1024 * 1024),
+    )(new_t, left, right, inv)
     return new_t.T, left, right
 
 

time: 78.7 us -> 87.1 us (1.11)
  Pallas kernels: 73.7 us -> 85 us
  local copies, waits for them, and re-layouts: 4.27 us -> 1.16 us
    pallas_call x1, Pallas kernels: 73.7 us -> 83.2 us  [shards(): pl.pallas_call(kernel, out_shape=(jax.ShapeDtypeStruct((COLS, ROWS), F32)...]
    unnamed x5 -> x2, local copies, waits for them, and re-layouts: 4.27 us -> 1.16 us
    pallas_call x0 -> x1, Pallas kernels: none -> 1.88 us  [shards(): pl.pallas_call(write_out, out_shape=(jax.ShapeDtypeStruct((COLS, ROWS), F...]
where the time goes in v2:
time: 87.1 us; the launch traced here: 87 us
  Pallas kernels  85 us (98%)
  local copies, waits for them, and re-layouts  1.16 us (1%)
    pallas_call x1, Pallas kernels, shards(): pl.pallas_call(kernel, out_shape=(jax.ShapeDtypeStruct((COLS, ROWS), F32)...  83.2 us
    pallas_call x1, Pallas kernels, shards(): pl.pallas_call(write_out, out_shape=(jax.ShapeDtypeStruct((COLS, ROWS), F...  1.88 us

profile of v2, /device:TPU:1, one launch (start us, length us, event | category | flops | bytes accessed | tf_op | source)
XLA Modules:
  0.0 87.0 jit_solution(2949295671356605412)
XLA Ops:
  0.6 0.0 copy-start
  0.6 1.2 %copy-done = f32[864,256]{1,0:T(8,128)S(1)} copy-done((f32[864,256]{1,0:T(8,128)S(1)}, f32[864,256]{1,0:T(8,128)}, u32[]{:S(2)}) %copy-start) | copy-done | bytes 884760
  1.8 83.2 %shard_map.67 = (f32[864,640]{1,0:T(8,128)S(1)}, f32[640,256]{1,0:T(8,128)S(1)}, f32[864,256]{1,0:T(8,128)S(1)}, f32[1,256]{1,0:T(1,128)S(1)}) custom-call(f32[864,640]{1,0:T(8,128)} %bitcast.4, bf16[2048,640]{1,0:T(8,128)(2,1)} %act_hbm.1, bf16[864,2048]{1,0:T(8,128)(2,1)} %bitcast.3, f32[864,256]{1,0:T(8,128)S(1)} %copy-done), custom_call_target="tpu_custom_call" | custom-call | tf_op jit(solution)/shard_map/pallas_call | solution.py:483
  85.0 1.9 %shard_map.68 = (f32[864,640]{1,0:T(8,128)}, f32[640,256]{1,0:T(8,128)}, f32[864,256]{1,0:T(8,128)}) custom-call(f32[864,640]{1,0:T(8,128)S(1)} %get-tuple-element.10.new, f32[640,256]{1,0:T(8,128)S(1)} %get-tuple-element.11.left, f32[864,256]{1,0:T(8,128)S(1)} %get-tuple-element.12.right, f32[1,256]{1,0:T(1,128)S(1)} %get-tuple-element.13.inv), custom_call_target="tpu_custom_call" | custom-call | tf_op jit(solution)/shard_map/pallas_call | solution.py:534
Async XLA Ops:
  0.6 1.2 %copy-start = (f32[864,256]{1,0:T(8,128)S(1)}, f32[864,256]{1,0:T(8,128)}, u32[]{:S(2)}) copy-start(f32[864,256]{1,0:T(8,128)} %basis_hbm.1) | copy-start | bytes 2654212

commit v3 on v1

--- a/solution.py
+++ b/solution.py
@@ -20,6 +20,7 @@
 COLS_PAD = 896
 STEP = 288
 GROUPS = ((0, 2), (2, 2), (4, 1))
+FAR_Z = (4, 3, 5, 2, 6, 1, 7)
 
 
 def mm(a, b, ca, cb):
@@ -98,12 +99,12 @@
     return joined(*inverse_factor_step(a[:64, :64], a[64:, :64], a[64:, 64:], inverse_factor_64))
 
 
-def kernel(mom_hbm, act_hbm, grad_hbm, basis_hbm, newm_hbm, left_hbm, newb_hbm,
+def kernel(mom_hbm, act_hbm, grad_hbm, basis_hbm, newm_hbm, left_hbm, newb_hbm, inv_hbm,
            grad, act, merged, basis, bt_hi, bt_lo, m_hi, m_lo,
-           part, from_y, mine, from_z, full,
+           part, from_y, from_z, full,
            gram, gram_pair, gram_x, gram_all,
            coef, coef_pair, coef_sum, coef_x, coef_all,
-           right, r_hi, r_lo, left, sq_z, sq_y,
+           right, r_hi, r_lo, left, sq, inv,
            send, recv, local):
     row, col = lax.axis_index("row"), lax.axis_index("col")
     x, core = row // 2, lax.rem(row, 2)
@@ -128,18 +129,23 @@
         pltpu.make_async_copy(grad_hbm.at[pl.ds(STEP * i, STEP)], grad.at[pl.ds(STEP * i, STEP)], local.at[3 + i])
         for i in range(3)
     ]
-    mom_load = pltpu.make_async_copy(mom_hbm, merged, local.at[6])
+    mom_load = [
+        pltpu.make_async_copy(mom_hbm.at[pl.ds(STEP * i, STEP)], merged.at[pl.ds(STEP * i, STEP)], local.at[8 + i])
+        for i in range(3)
+    ]
     basis_load = pltpu.make_async_copy(basis_hbm, basis.at[pl.ds(0, COLS)], local.at[7])
     basis_load.start()
     loads[0].start()
-    for c in grad_load:
-        c.start()
-    mom_load.start()
-    loads[1].start()
-    loads[2].start()
+    for i in range(2):
+        grad_load[i].start()
+        mom_load[i].start()
 
     barrier = pltpu.get_barrier_semaphore()
-    peers = [at_y(d) for d in range(1, YS)] + [at_z(d) for d in range(1, ZS)] + [at_x(d) for d in range(1, XS)] + [other]
+    same_row = [
+        (row, lax.rem(z + dz, ZS) * YS + lax.rem(y + dy, YS))
+        for dz in (4, 3, 5, 2, 6, 1, 7, 0) for dy in (2, 1, 3, 0) if dz or dy
+    ]
+    peers = same_row + [at_x(d) for d in range(1, XS)] + [other]
     for peer in peers:
         pl.semaphore_signal(barrier, inc=1, device_id=peer, device_id_type=MESH)
 
@@ -168,13 +174,8 @@
         t, n = GROUPS[g]
         lanes = slice(128 * t, 128 * (t + n))
         loads[g].wait()
-        if g == 0:
-            for c in grad_load:
-                c.wait()
-            mom_load.wait()
-
-        @pl.loop(0, COLS // STEP)
-        def _(i):
+
+        def merge(i):
             rows = pl.ds(pl.multiple_of(i * STEP, STEP), STEP)
             m = merged[rows, lanes] + mm16(grad[rows, :], act[:, lanes], 1, 0)
             merged[rows, lanes] = m
@@ -182,6 +183,19 @@
             m_hi[rows, lanes] = hi
             m_lo[rows, lanes] = lo
 
+        if g == 0:
+            for i in range(COLS // STEP):
+                grad_load[i].wait()
+                mom_load[i].wait()
+                if i == 0:
+                    grad_load[2].start()
+                    mom_load[2].start()
+                else:
+                    loads[i].start()
+                merge(i)
+        else:
+            pl.loop(0, COLS // STEP)(merge)
+
         p = mm3((bt_hi[...], bt_lo[...]), (m_hi[:, lanes], m_lo[:, lanes]), 1, 0)
         for k in range(n):
             part[t + k] = p[:, 128 * k:128 * k + 128]
@@ -192,37 +206,25 @@
     def mine_y(d):
         return pl.ds(pl.multiple_of(64 * lax.rem(y + d, YS), 64), 64)
 
-    def mine_z(d):
-        return pl.ds(pl.multiple_of(8 * lax.rem(z + d, ZS), 8), 8)
-
-    own = pl.ds(pl.multiple_of(64 * y + 8 * z, 8), 8)
-
     def scatter_y(g):
-        return [remote(part.at[span(g), mine_y(d)], from_y.at[d - 1, span(g)], at_y(d)) for d in range(1, YS)]
-
-    def scatter_z(g, before):
+        return [remote(part.at[span(g), mine_y(d)], from_y.at[d - 1, span(g)], at_y(d)) for d in (2, 1, 3)]
+
+    def share_z(g, before):
         for c in before:
             c.wait_recv()
         t, n = GROUPS[g]
         for k in range(t, t + n):
-            mine[k] = (part[k, mine_y(0), :] + from_y[0, k]) + (from_y[1, k] + from_y[2, k])
-        return [remote(mine.at[span(g), mine_z(d)], from_z.at[d - 1, span(g)], at_z(d)) for d in range(1, ZS)]
-
-    def gather_z(g, before):
+            from_z[z, k] = (part[k, mine_y(0), :] + from_y[0, k]) + (from_y[1, k] + from_y[2, k])
+        return [remote(from_z.at[z, span(g)], from_z.at[z, span(g)], at_z(d)) for d in FAR_Z]
+
+    def gather_y(g, before):
         for c in before:
             c.wait_recv()
         t, n = GROUPS[g]
         for k in range(t, t + n):
-            total = mine[k, mine_z(0), :]
-            for d in range(ZS - 1):
-                total = total + from_z[d, k]
-            full[k, own, :] = total
-        return [remote(full.at[span(g), own], full.at[span(g), own], at_z(d)) for d in range(1, ZS)]
-
-    def gather_y(g, before):
-        for c in before:
-            c.wait_recv()
-        return [remote(full.at[span(g), mine_y(0)], full.at[span(g), mine_y(0)], at_y(d)) for d in range(1, YS)]
+            v = [from_z[d, k] for d in range(ZS)]
+            full[k, mine_y(0), :] = ((v[0] + v[1]) + (v[2] + v[3])) + ((v[4] + v[5]) + (v[6] + v[7]))
+        return [remote(full.at[span(g), mine_y(0)], full.at[span(g), mine_y(0)], at_y(d)) for d in (2, 1, 3)]
 
     def whole(g):
         t, n = GROUPS[g]
@@ -246,26 +248,23 @@
     a0 = scatter_y(0)
     project(1)
     a1 = scatter_y(1)
-    b0 = scatter_z(0, a0)
+    b0 = share_z(0, a0)
     project(2)
     a2 = scatter_y(2)
-    b1 = scatter_z(1, a1)
-    c0 = gather_z(0, b0)
-    b2 = scatter_z(2, a2)
-    c1 = gather_z(1, b1)
-    d0 = gather_y(0, c0)
-    c2 = gather_z(2, b2)
-    d1 = gather_y(1, c1)
-    d2 = gather_y(2, c2)
-    for c in d0:
+    b1 = share_z(1, a1)
+    c0 = gather_y(0, b0)
+    b2 = share_z(2, a2)
+    for c in c0:
         c.wait_recv()
     gr = mm(whole(0), whole(0), 1, 1)
+    c1 = gather_y(1, b1)
     coefficients(0)
-    for c in d1:
+    c2 = gather_y(2, b2)
+    for c in c1:
         c.wait_recv()
     gr = gr + mm(whole(1), whole(1), 1, 1)
     coefficients(1)
-    for c in d2:
+    for c in c2:
         c.wait_recv()
     gr = gr + mm(whole(2), whole(2), 1, 1)
 
@@ -293,13 +292,13 @@
         return remote(gram_all.at[pl.ds(b, n), half], gram_all.at[pl.ds(b, n), half], other)
 
     f0 = gram_over_x(0, 1, e0)
-    f1 = gram_over_x(1, 2, e1)
 
     def coef_rows(d):
         return pl.ds(pl.multiple_of(216 * lax.rem(x + d, XS), 216), 216)
 
     h.wait_recv()
     coef_sum[...] = coef[core] + coef_pair[...]
+    f1 = gram_over_x(1, 2, e1)
     r = [remote(coef_sum.at[coef_rows(d)], coef_x.at[d - 1], at_x(d)) for d in range(1, XS)]
     g0 = gram_to_pair(0, 1, f0)
     g0.wait_recv()
@@ -345,8 +344,8 @@
         return squares + jnp.sum(c * c, axis=0, keepdims=True)
 
     squares = lax.fori_loop(0, COLS // STEP, finish, jnp.zeros((1, RANK), F32))
-    sq_z[z] = squares
-    n = [remote(sq_z.at[z], sq_z.at[z], at_z(d)) for d in range(1, ZS)]
+    sq[col] = squares
+    n = [remote(sq.at[col], sq.at[col], peer) for peer in same_row]
 
     outs = []
     for g, (t, num) in enumerate(GROUPS):
@@ -360,26 +359,20 @@
             rows = pl.ds(pl.multiple_of(i * STEP, STEP), STEP)
             merged[rows, lanes] = merged[rows, lanes] - 0.5 * mm3((r_hi[rows, :], r_lo[rows, :]), o, 1, 0)
 
-        if g == 1:
-            for c in n:
-                c.wait_recv()
-            total = sq_z[0]
-            for k in range(1, ZS):
-                total = total + sq_z[k]
-            sq_y[y] = total
-            v = [remote(sq_y.at[y], sq_y.at[y], at_y(d)) for d in range(1, YS)]
-        out = pltpu.make_async_copy(merged.at[:, lanes], newm_hbm.at[:, lanes], local.at[8 + g])
+        out = pltpu.make_async_copy(merged.at[:, lanes], newm_hbm.at[:, lanes], local.at[11 + g])
         out.start()
         outs.append(out)
-    out = pltpu.make_async_copy(left, left_hbm, local.at[11])
-    out.start()
-    outs.append(out)
-    for c in v:
-        c.wait_recv()
-    total = (sq_y[0] + sq_y[1]) + (sq_y[2] + sq_y[3])
-    inv = lax.rsqrt(total / F + EPS)
-    right[...] = right[...] * inv
-    out = pltpu.make_async_copy(right, newb_hbm, local.at[12])
+    for src, dst, i in ((left, left_hbm, 14), (right, newb_hbm, 15)):
+        out = pltpu.make_async_copy(src, dst, local.at[i])
+        out.start()
+        outs.append(out)
+    for c in n:
+        c.wait_recv()
+    total = sq[0]
+    for k in range(1, YS * ZS):
+        total = total + sq[k]
+    inv[...] = lax.rsqrt(total / F + EPS)
+    out = pltpu.make_async_copy(inv, inv_hbm, local.at[16])
     out.start()
     outs.append(out)
     for c in started:
@@ -388,20 +381,35 @@
         out.wait()
 
 
-COPIES = 3 * 20 + 10 + 8 + 10
+def write_out(new, left, right, inv, new_hbm, left_hbm, right_hbm, scaled, sems):
+    outs = [
+        pltpu.make_async_copy(new, new_hbm, sems.at[0]),
+        pltpu.make_async_copy(left, left_hbm, sems.at[1]),
+        pltpu.make_async_copy(scaled, right_hbm, sems.at[2]),
+    ]
+    outs[0].start()
+    outs[1].start()
+    scaled[...] = right[...] * inv[...]
+    outs[2].start()
+    for out in outs:
+        out.wait()
+
+
+COPIES = 3 * 13 + 10 + 8 + 31
 
 
 def shards(momentum, activations, out_grads, basis):
     any_ = pl.BlockSpec(memory_space=pl.ANY)
-    new_t, left, right = pl.pallas_call(
+    new_t, left, right, inv = pl.pallas_call(
         kernel,
         out_shape=(
             jax.ShapeDtypeStruct((COLS, ROWS), F32),
             jax.ShapeDtypeStruct((ROWS, RANK), F32),
             jax.ShapeDtypeStruct((COLS, RANK), F32),
+            jax.ShapeDtypeStruct((1, RANK), F32),
         ),
-        in_specs=[any_] * 4,
-        out_specs=[any_] * 3,
+        in_specs=[pl.BlockSpec(memory_space=pltpu.HBM)] * 4,
+        out_specs=[any_] * 4,
         scratch_shapes=[
             pltpu.VMEM((COLS, TOKENS), BF16),
             pltpu.VMEM((TOKENS, ROWS), BF16),
@@ -413,8 +421,7 @@
             pltpu.VMEM((COLS_PAD, ROWS), BF16),
             pltpu.VMEM((5, RANK, 128), F32),
             pltpu.VMEM((YS - 1, 5, 64, 128), F32),
-            pltpu.VMEM((5, 64, 128), F32),
-            pltpu.VMEM((ZS - 1, 5, 8, 128), F32),
+            pltpu.VMEM((ZS, 5, 64, 128), F32),
             pltpu.VMEM((5, RANK, 128), F32),
             pltpu.VMEM((3, 128, 128), F32),
             pltpu.VMEM((3, 64, 128), F32),
@@ -429,15 +436,28 @@
             pltpu.VMEM((COLS, RANK), BF16),
             pltpu.VMEM((COLS, RANK), BF16),
             pltpu.VMEM((ROWS, RANK), F32),
-            pltpu.VMEM((ZS, 1, RANK), F32),
-            pltpu.VMEM((YS, 1, RANK), F32),
+            pltpu.VMEM((YS * ZS, 1, RANK), F32),
+            pltpu.VMEM((1, RANK), F32),
             pltpu.SemaphoreType.DMA((COPIES,)),
             pltpu.SemaphoreType.DMA((COPIES,)),
-            pltpu.SemaphoreType.DMA((13,)),
+            pltpu.SemaphoreType.DMA((17,)),
         ],
         compiler_params=pltpu.CompilerParams(
             collective_id=0, has_side_effects=True, vmem_limit_bytes=48 * 1024 * 1024),
     )(momentum.T, activations, out_grads.T, basis)
+    vmem = pl.BlockSpec(memory_space=pltpu.VMEM)
+    new_t, left, right = pl.pallas_call(
+        write_out,
+        out_shape=(
+            jax.ShapeDtypeStruct((COLS, ROWS), F32),
+            jax.ShapeDtypeStruct((ROWS, RANK), F32),
+            jax.ShapeDtypeStruct((COLS, RANK), F32),
+        ),
+        in_specs=[any_, any_, vmem, vmem],
+        out_specs=[any_] * 3,
+        scratch_shapes=[pltpu.VMEM((COLS, RANK), F32), pltpu.SemaphoreType.DMA((3,))],
+        compiler_params=pltpu.CompilerParams(vmem_limit_bytes=8 * 1024 * 1024),
+    )(new_t, left, right, inv)
     return new_t.T, left, right
 
 

time: 78.7 us -> 90.2 us (1.15)
  Pallas kernels: 73.7 us -> 88.1 us
  local copies, waits for them, and re-layouts: 4.27 us -> 1.16 us
    pallas_call x1, Pallas kernels: 73.7 us -> 86.2 us  [shards(): pl.pallas_call(kernel, out_shape=(jax.ShapeDtypeStruct((COLS, ROWS), F32)...]
    unnamed x5 -> x2, local copies, waits for them, and re-layouts: 4.27 us -> 1.16 us
    pallas_call x0 -> x1, Pallas kernels: none -> 1.88 us  [shards(): pl.pallas_call(write_out, out_shape=(jax.ShapeDtypeStruct((COLS, ROWS), F...]
where the time goes in v3:
time: 90.2 us; the launch traced here: 90.1 us
  Pallas kernels  88.1 us (98%)
  local copies, waits for them, and re-layouts  1.16 us (1%)
    pallas_call x1, Pallas kernels, shards(): pl.pallas_call(kernel, out_shape=(jax.ShapeDtypeStruct((COLS, ROWS), F32)...  86.2 us
    pallas_call x1, Pallas kernels, shards(): pl.pallas_call(write_out, out_shape=(jax.ShapeDtypeStruct((COLS, ROWS), F...  1.88 us

profile of v3, /device:TPU:1, one launch (start us, length us, event | category | flops | bytes accessed | tf_op | source)
XLA Modules:
  0.0 90.1 jit_solution(4991492962223200683)
XLA Ops:
  0.6 0.0 copy-start
  0.6 1.2 %copy-done = f32[864,256]{1,0:T(8,128)S(1)} copy-done((f32[864,256]{1,0:T(8,128)S(1)}, f32[864,256]{1,0:T(8,128)}, u32[]{:S(2)}) %copy-start) | copy-done | bytes 884760
  1.8 86.2 %shard_map.67 = (f32[864,640]{1,0:T(8,128)S(1)}, f32[640,256]{1,0:T(8,128)S(1)}, f32[864,256]{1,0:T(8,128)S(1)}, f32[1,256]{1,0:T(1,128)S(1)}) custom-call(f32[864,640]{1,0:T(8,128)} %bitcast.4, bf16[2048,640]{1,0:T(8,128)(2,1)} %act_hbm.1, bf16[864,2048]{1,0:T(8,128)(2,1)} %bitcast.3, f32[864,256]{1,0:T(8,128)S(1)} %copy-done), custom_call_target="tpu_custom_call" | custom-call | tf_op jit(solution)/shard_map/pallas_call | solution.py:403
  88.0 1.9 %shard_map.68 = (f32[864,640]{1,0:T(8,128)}, f32[640,256]{1,0:T(8,128)}, f32[864,256]{1,0:T(8,128)}) custom-call(f32[864,640]{1,0:T(8,128)S(1)} %get-tuple-element.10.new, f32[640,256]{1,0:T(8,128)S(1)} %get-tuple-element.11.left, f32[864,256]{1,0:T(8,128)S(1)} %get-tuple-element.12.right, f32[1,256]{1,0:T(1,128)S(1)} %get-tuple-element.13.inv), custom_call_target="tpu_custom_call" | custom-call | tf_op jit(solution)/shard_map/pallas_call | solution.py:449
Async XLA Ops:
  0.6 1.2 %copy-start = (f32[864,256]{1,0:T(8,128)S(1)}, f32[864,256]{1,0:T(8,128)}, u32[]{:S(2)}) copy-start(f32[864,256]{1,0:T(8,128)} %basis_hbm.1) | copy-start | bytes 2654212

commit v4 on v1

--- a/solution.py
+++ b/solution.py
@@ -20,6 +20,7 @@
 COLS_PAD = 896
 STEP = 288
 GROUPS = ((0, 2), (2, 2), (4, 1))
+CHUNKS = ((0, 448), (448, 416))
 
 
 def mm(a, b, ca, cb):
@@ -98,12 +99,12 @@
     return joined(*inverse_factor_step(a[:64, :64], a[64:, :64], a[64:, 64:], inverse_factor_64))
 
 
-def kernel(mom_hbm, act_hbm, grad_hbm, basis_hbm, newm_hbm, left_hbm, newb_hbm,
+def kernel(mom_hbm, act_hbm, grad_hbm, basis_hbm, newm_hbm, left_hbm, newb_hbm, inv_hbm,
            grad, act, merged, basis, bt_hi, bt_lo, m_hi, m_lo,
            part, from_y, mine, from_z, full,
            gram, gram_pair, gram_x, gram_all,
            coef, coef_pair, coef_sum, coef_x, coef_all,
-           right, r_hi, r_lo, left, sq_z, sq_y,
+           right, r_hi, r_lo, left, sq_z, sq_y, inv,
            send, recv, local):
     row, col = lax.axis_index("row"), lax.axis_index("col")
     x, core = row // 2, lax.rem(row, 2)
@@ -173,9 +174,9 @@
                 c.wait()
             mom_load.wait()
 
-        @pl.loop(0, COLS // STEP)
+        @pl.loop(0, 2)
         def _(i):
-            rows = pl.ds(pl.multiple_of(i * STEP, STEP), STEP)
+            rows = pl.ds(pl.multiple_of(i * (COLS // 2), COLS // 2), COLS // 2)
             m = merged[rows, lanes] + mm16(grad[rows, :], act[:, lanes], 1, 0)
             merged[rows, lanes] = m
             hi, lo = halves(m)
@@ -240,6 +241,13 @@
             for k in range(2):
                 v = c[:, 128 * k:128 * k + 128]
                 coef[k, rows, :] = v if g == 0 else coef[k, rows, :] + v
+
+    def last_coefficients(first, size):
+        t, n = GROUPS[2]
+        lanes, rows = slice(128 * t, 128 * (t + n)), slice(first, first + size)
+        c = mm3((m_hi[rows, lanes], m_lo[rows, lanes]), halves(whole(2)), 1, 1)
+        for k in range(2):
+            coef[k, rows, :] = coef[k, rows, :] + c[:, 128 * k:128 * k + 128]
 
     project(0)
     pl.semaphore_wait(barrier, len(peers))
@@ -276,9 +284,6 @@
     other_half = pl.ds(pl.multiple_of(64 * (1 - core), 64), 64)
     e0 = remote(gram.at[pl.ds(0, 1), other_half], gram_pair.at[pl.ds(0, 1)], other)
     e1 = remote(gram.at[pl.ds(1, 2), other_half], gram_pair.at[pl.ds(1, 2)], other)
-    coefficients(2)
-    h = remote(coef.at[1 - core], coef_pair, other)
-
     def gram_over_x(b, n, before):
         before.wait_recv()
         for k in range(b, b + n):
@@ -292,15 +297,41 @@
             gram_all[k, half, :] = (gram_x[0, k] + gram_x[1, k]) + (gram_x[2, k] + gram_x[3, k])
         return remote(gram_all.at[pl.ds(b, n), half], gram_all.at[pl.ds(b, n), half], other)
 
+    def chunk(c):
+        return pl.ds(*CHUNKS[c])
+
+    def quarter(c, d):
+        first, size = CHUNKS[c]
+        return pl.ds(pl.multiple_of(first + size // XS * lax.rem(x + d, XS), 8), size // XS)
+
+    def coef_over_x(c, before):
+        before.wait_recv()
+        coef_sum[chunk(c)] = coef[core, chunk(c), :] + coef_pair[chunk(c)]
+        size = CHUNKS[c][1] // XS
+        return [
+            remote(coef_sum.at[quarter(c, d)], coef_x.at[d - 1, pl.ds(112 * c, size)], at_x(d)) for d in (2, 1, 3)
+        ]
+
+    def coef_gather(c, before):
+        for copy in before:
+            copy.wait_recv()
+        own, got = quarter(c, 0), pl.ds(112 * c, CHUNKS[c][1] // XS)
+        coef_all[core, own, :] = (coef_sum[own, :] + coef_x[0, got, :]) + (coef_x[1, got, :] + coef_x[2, got, :])
+        return [remote(coef_all.at[core, own], coef_all.at[core, own], at_x(d)) for d in (2, 1, 3)]
+
+    def coef_to_pair(c, before):
+        for copy in before:
+            copy.wait_recv()
+        return remote(coef_all.at[core, chunk(c)], coef_all.at[core, chunk(c)], other)
+
+    last_coefficients(*CHUNKS[0])
+    h0 = remote(coef.at[1 - core, chunk(0)], coef_pair.at[chunk(0)], other)
     f0 = gram_over_x(0, 1, e0)
+    last_coefficients(*CHUNKS[1])
+    h1 = remote(coef.at[1 - core, chunk(1)], coef_pair.at[chunk(1)], other)
     f1 = gram_over_x(1, 2, e1)
-
-    def coef_rows(d):
-        return pl.ds(pl.multiple_of(216 * lax.rem(x + d, XS), 216), 216)
-
-    h.wait_recv()
-    coef_sum[...] = coef[core] + coef_pair[...]
-    r = [remote(coef_sum.at[coef_rows(d)], coef_x.at[d - 1], at_x(d)) for d in range(1, XS)]
+    r0 = coef_over_x(0, h0)
+    r1 = coef_over_x(1, h1)
     g0 = gram_to_pair(0, 1, f0)
     g0.wait_recv()
     a11 = gram_all[0]
@@ -309,30 +340,28 @@
     s = a11[64:, 64:] - mm(l21, l21, 1, 1)
     lw = mm(l21, w11, 1, 0)
     g1 = gram_to_pair(1, 2, f1)
+    q0 = coef_gather(0, r0)
     w22 = inverse_factor_64(s)
     wa = joined(w11, -mm(w22, lw, 1, 0), w22)
     g1.wait_recv()
+    q1 = coef_gather(1, r1)
     a22 = gram_all[2]
     l21 = mm(gram_all[1], wa, 1, 1)
     s = a22 - mm(l21, l21, 1, 1)
     lwa = mm(l21, wa, 1, 0)
-    for c in r:
-        c.wait_recv()
-    coef_all[core, coef_rows(0), :] = (coef_sum[coef_rows(0), :] + coef_x[0]) + (coef_x[1] + coef_x[2])
-    q = [remote(coef_all.at[core, coef_rows(0)], coef_all.at[core, coef_rows(0)], at_x(d)) for d in range(1, XS)]
     w11 = inverse_factor_64(s[:64, :64])
     l21 = mm(s[64:, :64], w11, 1, 1)
     s2 = s[64:, 64:] - mm(l21, l21, 1, 1)
     lw = mm(l21, w11, 1, 0)
-    for c in q:
-        c.wait_recv()
-    k0 = remote(coef_all.at[core], coef_all.at[core], other)
+    k0 = coef_to_pair(0, q0)
     w22 = inverse_factor_64(s2)
+    k1 = coef_to_pair(1, q1)
     wb = joined(w11, -mm(w22, lw, 1, 0), w22)
     w = joined(wa, -mm(wb, lwa, 1, 0), wb)
 
+    w_parts = halves(w)
     k0.wait_recv()
-    w_parts = halves(w)
+    k1.wait_recv()
 
     def finish(i, squares):
         rows = pl.ds(pl.multiple_of(i * STEP, STEP), STEP)
@@ -368,18 +397,17 @@
                 total = total + sq_z[k]
             sq_y[y] = total
             v = [remote(sq_y.at[y], sq_y.at[y], at_y(d)) for d in range(1, YS)]
-        out = pltpu.make_async_copy(merged.at[:, lanes], newm_hbm.at[:, lanes], local.at[8 + g])
+        out = pltpu.make_async_copy(merged.at[:, lanes], newm_hbm.at[:, lanes], local.at[11 + g])
         out.start()
         outs.append(out)
-    out = pltpu.make_async_copy(left, left_hbm, local.at[11])
-    out.start()
-    outs.append(out)
+    for src, dst, i in ((left, left_hbm, 14), (right, newb_hbm, 15)):
+        out = pltpu.make_async_copy(src, dst, local.at[i])
+        out.start()
+        outs.append(out)
     for c in v:
         c.wait_recv()
-    total = (sq_y[0] + sq_y[1]) + (sq_y[2] + sq_y[3])
-    inv = lax.rsqrt(total / F + EPS)
-    right[...] = right[...] * inv
-    out = pltpu.make_async_copy(right, newb_hbm, local.at[12])
+    inv[...] = lax.rsqrt(((sq_y[0] + sq_y[1]) + (sq_y[2] + sq_y[3])) / F + EPS)
+    out = pltpu.make_async_copy(inv, inv_hbm, local.at[16])
     out.start()
     outs.append(out)
     for c in started:
@@ -388,20 +416,35 @@
         out.wait()
 
 
-COPIES = 3 * 20 + 10 + 8 + 10
+def write_out(new, left, right, inv, new_hbm, left_hbm, right_hbm, scaled, sems):
+    outs = [
+        pltpu.make_async_copy(new, new_hbm, sems.at[0]),
+        pltpu.make_async_copy(left, left_hbm, sems.at[1]),
+        pltpu.make_async_copy(scaled, right_hbm, sems.at[2]),
+    ]
+    outs[0].start()
+    outs[1].start()
+    scaled[...] = right[...] * inv[...]
+    outs[2].start()
+    for out in outs:
+        out.wait()
+
+
+COPIES = 3 * 20 + 10 + 16 + 10
 
 
 def shards(momentum, activations, out_grads, basis):
     any_ = pl.BlockSpec(memory_space=pl.ANY)
-    new_t, left, right = pl.pallas_call(
+    new_t, left, right, inv = pl.pallas_call(
         kernel,
         out_shape=(
             jax.ShapeDtypeStruct((COLS, ROWS), F32),
             jax.ShapeDtypeStruct((ROWS, RANK), F32),
             jax.ShapeDtypeStruct((COLS, RANK), F32),
+            jax.ShapeDtypeStruct((1, RANK), F32),
         ),
-        in_specs=[any_] * 4,
-        out_specs=[any_] * 3,
+        in_specs=[pl.BlockSpec(memory_space=pltpu.HBM)] * 4,
+        out_specs=[any_] * 4,
         scratch_shapes=[
             pltpu.VMEM((COLS, TOKENS), BF16),
             pltpu.VMEM((TOKENS, ROWS), BF16),
@@ -431,13 +474,27 @@
             pltpu.VMEM((ROWS, RANK), F32),
             pltpu.VMEM((ZS, 1, RANK), F32),
             pltpu.VMEM((YS, 1, RANK), F32),
+            pltpu.VMEM((1, RANK), F32),
             pltpu.SemaphoreType.DMA((COPIES,)),
             pltpu.SemaphoreType.DMA((COPIES,)),
-            pltpu.SemaphoreType.DMA((13,)),
+            pltpu.SemaphoreType.DMA((17,)),
         ],
         compiler_params=pltpu.CompilerParams(
             collective_id=0, has_side_effects=True, vmem_limit_bytes=48 * 1024 * 1024),
     )(momentum.T, activations, out_grads.T, basis)
+    vmem = pl.BlockSpec(memory_space=pltpu.VMEM)
+    new_t, left, right = pl.pallas_call(
+        write_out,
+        out_shape=(
+            jax.ShapeDtypeStruct((COLS, ROWS), F32),
+            jax.ShapeDtypeStruct((ROWS, RANK), F32),
+            jax.ShapeDtypeStruct((COLS, RANK), F32),
+        ),
+        in_specs=[any_, any_, vmem, vmem],
+        out_specs=[any_] * 3,
+        scratch_shapes=[pltpu.VMEM((COLS, RANK), F32), pltpu.SemaphoreType.DMA((3,))],
+        compiler_params=pltpu.CompilerParams(vmem_limit_bytes=8 * 1024 * 1024),
+    )(new_t, left, right, inv)
     return new_t.T, left, right
 
 

time: 78.7 us -> 73.3 us (0.931)
  local copies, waits for them, and re-layouts: 4.27 us -> 1.16 us
  Pallas kernels: 73.7 us -> 71.4 us
    pallas_call x1, Pallas kernels: 73.7 us -> 69.5 us  [shards(): pl.pallas_call(kernel, out_shape=(jax.ShapeDtypeStruct((COLS, ROWS), F32)...]
    unnamed x5 -> x2, local copies, waits for them, and re-layouts: 4.27 us -> 1.16 us
    pallas_call x0 -> x1, Pallas kernels: none -> 1.88 us  [shards(): pl.pallas_call(write_out, out_shape=(jax.ShapeDtypeStruct((COLS, ROWS), F...]
where the time goes in v4:
time: 73.3 us; the launch traced here: 73.2 us
  Pallas kernels  71.4 us (97%)
  local copies, waits for them, and re-layouts  1.16 us (2%)
    pallas_call x1, Pallas kernels, shards(): pl.pallas_call(kernel, out_shape=(jax.ShapeDtypeStruct((COLS, ROWS), F32)...  69.5 us
    pallas_call x1, Pallas kernels, shards(): pl.pallas_call(write_out, out_shape=(jax.ShapeDtypeStruct((COLS, ROWS), F...  1.88 us

profile of v4, /device:TPU:1, one launch (start us, length us, event | category | flops | bytes accessed | tf_op | source)
XLA Modules:
  0.0 73.2 jit_solution(15217820274101597201)
XLA Ops:
  0.6 0.0 copy-start
  0.6 1.2 %copy-done = f32[864,256]{1,0:T(8,128)S(1)} copy-done((f32[864,256]{1,0:T(8,128)S(1)}, f32[864,256]{1,0:T(8,128)}, u32[]{:S(2)}) %copy-start) | copy-done | bytes 884760
  1.8 69.5 %shard_map.67 = (f32[864,640]{1,0:T(8,128)S(1)}, f32[640,256]{1,0:T(8,128)S(1)}, f32[864,256]{1,0:T(8,128)S(1)}, f32[1,256]{1,0:T(1,128)S(1)}) custom-call(f32[864,640]{1,0:T(8,128)} %bitcast.4, bf16[2048,640]{1,0:T(8,128)(2,1)} %act_hbm.1, bf16[864,2048]{1,0:T(8,128)(2,1)} %bitcast.3, f32[864,256]{1,0:T(8,128)S(1)} %copy-done), custom_call_target="tpu_custom_call" | custom-call | tf_op jit(solution)/shard_map/pallas_call | solution.py:438
  71.3 1.9 %shard_map.68 = (f32[864,640]{1,0:T(8,128)}, f32[640,256]{1,0:T(8,128)}, f32[864,256]{1,0:T(8,128)}) custom-call(f32[864,640]{1,0:T(8,128)S(1)} %get-tuple-element.10.new, f32[640,256]{1,0:T(8,128)S(1)} %get-tuple-element.11.left, f32[864,256]{1,0:T(8,128)S(1)} %get-tuple-element.12.right, f32[1,256]{1,0:T(1,128)S(1)} %get-tuple-element.13.inv), custom_call_target="tpu_custom_call" | custom-call | tf_op jit(solution)/shard_map/pallas_call | solution.py:486
Async XLA Ops:
  0.6 1.2 %copy-start = (f32[864,256]{1,0:T(8,128)S(1)}, f32[864,256]{1,0:T(8,128)}, u32[]{:S(2)}) copy-start(f32[864,256]{1,0:T(8,128)} %basis_hbm.1) | copy-start | bytes 2654212

commit v5 on v4

--- a/solution.py
+++ b/solution.py
@@ -46,7 +46,7 @@
 def row_of(v, r):
     return jnp.broadcast_to(v[r:r + 1, :], v.shape)
 
-def inverse_factor_64(block):
+def inverse_factor_64(block, halfway=None):
     r64 = lax.broadcasted_iota(jnp.int32, (64, 64), 0)
     c64 = lax.broadcasted_iota(jnp.int32, (64, 64), 1)
     eye = jnp.where(r64 == c64, 1.0, 0.0).astype(jnp.float32)
@@ -55,20 +55,28 @@
     sub = lax.broadcasted_iota(jnp.int32, (8, 128), 0)
     out = []
     for k in range(8):
+        if k == 4 and halfway is not None:
+            halfway()
         cols = [lane_of(t[k], 8 * k + c) for c in range(8)]
         e = [[row_of(cols[c], r) if r >= c else None for c in range(8)] for r in range(8)]
         rows = [row_of(t[k], r) for r in range(8)]
         rs = [None] * 8
         l = [[None] * 8 for _ in range(8)]
-        for c in range(8):
-            rs[c] = lax.rsqrt(e[c][c])
+        for c in range(0, 8, 2):
+            d = c + 1
+            p, q, v = e[c][c], e[d][c], e[d][d]
+            rs[c] = lax.rsqrt(p)
+            rs[d] = lax.rsqrt(p * v - q * q) * (p * rs[c])
             rows[c] = rows[c] * rs[c]
             for r in range(c + 1, 8):
                 l[r][c] = e[r][c] * rs[c]
-            for r in range(c + 1, 8):
-                for m in range(c + 1, r + 1):
-                    e[r][m] = e[r][m] - l[r][c] * l[m][c]
-                rows[r] = rows[r] - l[r][c] * rows[c]
+            rows[d] = (rows[d] - l[d][c] * rows[c]) * rs[d]
+            for r in range(d + 1, 8):
+                l[r][d] = (e[r][d] - l[r][c] * l[d][c]) * rs[d]
+            for r in range(d + 1, 8):
+                for m in range(d + 1, r + 1):
+                    e[r][m] = e[r][m] - l[r][c] * l[m][c] - l[r][d] * l[m][d]
+                rows[r] = rows[r] - l[r][c] * rows[c] - l[r][d] * rows[d]
         u = rows[0]
         for c in range(1, 8):
             u = jnp.where(sub == c, rows[c], u)
@@ -277,6 +285,7 @@
         c.wait_recv()
     gr = gr + mm(whole(2), whole(2), 1, 1)
 
+    gr = gr * F32(2.0 ** -30)
     gram[0] = gr[:128, :128]
     gram[1] = gr[128:, :128]
     gram[2] = gr[128:, 128:]
@@ -341,10 +350,10 @@
     lw = mm(l21, w11, 1, 0)
     g1 = gram_to_pair(1, 2, f1)
     q0 = coef_gather(0, r0)
-    w22 = inverse_factor_64(s)
+    q1 = []
+    w22 = inverse_factor_64(s, lambda: q1.extend(coef_gather(1, r1)))
     wa = joined(w11, -mm(w22, lw, 1, 0), w22)
     g1.wait_recv()
-    q1 = coef_gather(1, r1)
     a22 = gram_all[2]
     l21 = mm(gram_all[1], wa, 1, 1)
     s = a22 - mm(l21, l21, 1, 1)
@@ -354,14 +363,14 @@
     s2 = s[64:, 64:] - mm(l21, l21, 1, 1)
     lw = mm(l21, w11, 1, 0)
     k0 = coef_to_pair(0, q0)
-    w22 = inverse_factor_64(s2)
-    k1 = coef_to_pair(1, q1)
+    k1 = []
+    w22 = inverse_factor_64(s2, lambda: k1.append(coef_to_pair(1, q1)))
     wb = joined(w11, -mm(w22, lw, 1, 0), w22)
     w = joined(wa, -mm(wb, lwa, 1, 0), wb)
 
-    w_parts = halves(w)
+    w_parts = halves(w * F32(2.0 ** -15))
     k0.wait_recv()
-    k1.wait_recv()
+    k1[0].wait_recv()
 
     def finish(i, squares):
         rows = pl.ds(pl.multiple_of(i * STEP, STEP), STEP)

time: 73.3 us -> 72.4 us (0.988)
  Pallas kernels: 71.4 us -> 70.5 us
    pallas_call x1, Pallas kernels: 69.5 us -> 68.6 us  [shards(): pl.pallas_call(kernel, out_shape=(jax.ShapeDtypeStruct((COLS, ROWS), F32)...]
where the time goes in v5:
time: 72.4 us; the launch traced here: 72.3 us
  Pallas kernels  70.5 us (97%)
  local copies, waits for them, and re-layouts  1.16 us (2%)
    pallas_call x1, Pallas kernels, shards(): pl.pallas_call(kernel, out_shape=(jax.ShapeDtypeStruct((COLS, ROWS), F32)...  68.6 us
    pallas_call x1, Pallas kernels, shards(): pl.pallas_call(write_out, out_shape=(jax.ShapeDtypeStruct((COLS, ROWS), F...  1.88 us

profile of v5, /device:TPU:1, one launch (start us, length us, event | category | flops | bytes accessed | tf_op | source)
XLA Modules:
  0.0 72.3 jit_solution(5390456564125861994)
XLA Ops:
  0.6 0.0 copy-start
  0.6 1.2 %copy-done = f32[864,256]{1,0:T(8,128)S(1)} copy-done((f32[864,256]{1,0:T(8,128)S(1)}, f32[864,256]{1,0:T(8,128)}, u32[]{:S(2)}) %copy-start) | copy-done | bytes 884760
  1.8 68.6 %shard_map.67 = (f32[864,640]{1,0:T(8,128)S(1)}, f32[640,256]{1,0:T(8,128)S(1)}, f32[864,256]{1,0:T(8,128)S(1)}, f32[1,256]{1,0:T(1,128)S(1)}) custom-call(f32[864,640]{1,0:T(8,128)} %bitcast.4, bf16[2048,640]{1,0:T(8,128)(2,1)} %act_hbm.1, bf16[864,2048]{1,0:T(8,128)(2,1)} %bitcast.3, f32[864,256]{1,0:T(8,128)S(1)} %copy-done), custom_call_target="tpu_custom_call" | custom-call | tf_op jit(solution)/shard_map/pallas_call | solution.py:447
  70.4 1.9 %shard_map.68 = (f32[864,640]{1,0:T(8,128)}, f32[640,256]{1,0:T(8,128)}, f32[864,256]{1,0:T(8,128)}) custom-call(f32[864,640]{1,0:T(8,128)S(1)} %get-tuple-element.10.new, f32[640,256]{1,0:T(8,128)S(1)} %get-tuple-element.11.left, f32[864,256]{1,0:T(8,128)S(1)} %get-tuple-element.12.right, f32[1,256]{1,0:T(1,128)S(1)} %get-tuple-element.13.inv), custom_call_target="tpu_custom_call" | custom-call | tf_op jit(solution)/shard_map/pallas_call | solution.py:495
Async XLA Ops:
  0.6 1.2 %copy-start = (f32[864,256]{1,0:T(8,128)S(1)}, f32[864,256]{1,0:T(8,128)}, u32[]{:S(2)}) copy-start(f32[864,256]{1,0:T(8,128)} %basis_hbm.1) | copy-start | bytes 2654212

commit v6 on v5

--- a/solution.py
+++ b/solution.py
@@ -107,12 +107,12 @@
     return joined(*inverse_factor_step(a[:64, :64], a[64:, :64], a[64:, 64:], inverse_factor_64))
 
 
-def kernel(mom_hbm, act_hbm, grad_hbm, basis_hbm, newm_hbm, left_hbm, newb_hbm, inv_hbm,
+def kernel(mom_hbm, act_hbm, grad_hbm, basis_hbm, newm_hbm, left_hbm, newb_hbm, inv_ref,
            grad, act, merged, basis, bt_hi, bt_lo, m_hi, m_lo,
            part, from_y, mine, from_z, full,
            gram, gram_pair, gram_x, gram_all,
            coef, coef_pair, coef_sum, coef_x, coef_all,
-           right, r_hi, r_lo, left, sq_z, sq_y, inv,
+           right, r_hi, r_lo, left, sq_z, sq_y,
            send, recv, local):
     row, col = lax.axis_index("row"), lax.axis_index("col")
     x, core = row // 2, lax.rem(row, 2)
@@ -338,8 +338,8 @@
     f0 = gram_over_x(0, 1, e0)
     last_coefficients(*CHUNKS[1])
     h1 = remote(coef.at[1 - core, chunk(1)], coef_pair.at[chunk(1)], other)
+    r0 = coef_over_x(0, h0)
     f1 = gram_over_x(1, 2, e1)
-    r0 = coef_over_x(0, h0)
     r1 = coef_over_x(1, h1)
     g0 = gram_to_pair(0, 1, f0)
     g0.wait_recv()
@@ -373,7 +373,7 @@
     k1[0].wait_recv()
 
     def finish(i, squares):
-        rows = pl.ds(pl.multiple_of(i * STEP, STEP), STEP)
+        rows = pl.ds(pl.multiple_of(i * (COLS // 2), COLS // 2), COLS // 2)
         c = jnp.concatenate([coef_all[0, rows, :], coef_all[1, rows, :]], axis=1)
         c = mm3(halves(c), w_parts, 1, 1)
         right[rows, :] = c
@@ -382,7 +382,7 @@
         r_lo[rows, :] = lo
         return squares + jnp.sum(c * c, axis=0, keepdims=True)
 
-    squares = lax.fori_loop(0, COLS // STEP, finish, jnp.zeros((1, RANK), F32))
+    squares = lax.fori_loop(0, 2, finish, jnp.zeros((1, RANK), F32))
     sq_z[z] = squares
     n = [remote(sq_z.at[z], sq_z.at[z], at_z(d)) for d in range(1, ZS)]
 
@@ -415,10 +415,7 @@
         outs.append(out)
     for c in v:
         c.wait_recv()
-    inv[...] = lax.rsqrt(((sq_y[0] + sq_y[1]) + (sq_y[2] + sq_y[3])) / F + EPS)
-    out = pltpu.make_async_copy(inv, inv_hbm, local.at[16])
-    out.start()
-    outs.append(out)
+    inv_ref[...] = lax.rsqrt(((sq_y[0] + sq_y[1]) + (sq_y[2] + sq_y[3])) / F + EPS)
     for c in started:
         c.wait_send()
     for out in outs:
@@ -453,7 +450,7 @@
             jax.ShapeDtypeStruct((1, RANK), F32),
         ),
         in_specs=[pl.BlockSpec(memory_space=pltpu.HBM)] * 4,
-        out_specs=[any_] * 4,
+        out_specs=[any_] * 3 + [pl.BlockSpec(memory_space=pltpu.VMEM)],
         scratch_shapes=[
             pltpu.VMEM((COLS, TOKENS), BF16),
             pltpu.VMEM((TOKENS, ROWS), BF16),
@@ -483,7 +480,6 @@
             pltpu.VMEM((ROWS, RANK), F32),
             pltpu.VMEM((ZS, 1, RANK), F32),
             pltpu.VMEM((YS, 1, RANK), F32),
-            pltpu.VMEM((1, RANK), F32),
             pltpu.SemaphoreType.DMA((COPIES,)),
             pltpu.SemaphoreType.DMA((COPIES,)),
             pltpu.SemaphoreType.DMA((17,)),

time: 72.4 us -> 72 us (level)
  no operation moved by 1% of the time
where the time goes in v6:
time: 72 us; the launch traced here: 71.8 us
  Pallas kernels  70 us (97%)
  local copies, waits for them, and re-layouts  1.16 us (2%)
    pallas_call x1, Pallas kernels, shards(): pl.pallas_call(kernel, out_shape=(jax.ShapeDtypeStruct((COLS, ROWS), F32)...  68.1 us
    pallas_call x1, Pallas kernels, shards(): pl.pallas_call(write_out, out_shape=(jax.ShapeDtypeStruct((COLS, ROWS), F...  1.88 us

profile of v6, /device:TPU:1, one launch (start us, length us, event | category | flops | bytes accessed | tf_op | source)
XLA Modules:
  0.0 71.8 jit_solution(17347026735765936166)
XLA Ops:
  0.6 0.0 copy-start
  0.6 1.2 %copy-done = f32[864,256]{1,0:T(8,128)S(1)} copy-done((f32[864,256]{1,0:T(8,128)S(1)}, f32[864,256]{1,0:T(8,128)}, u32[]{:S(2)}) %copy-start) | copy-done | bytes 884760
  1.8 68.1 %shard_map.67 = (f32[864,640]{1,0:T(8,128)S(1)}, f32[640,256]{1,0:T(8,128)S(1)}, f32[864,256]{1,0:T(8,128)S(1)}, f32[1,256]{1,0:T(1,128)S(1)}) custom-call(f32[864,640]{1,0:T(8,128)} %bitcast.4, bf16[2048,640]{1,0:T(8,128)(2,1)} %act_hbm.1, bf16[864,2048]{1,0:T(8,128)(2,1)} %bitcast.3, f32[864,256]{1,0:T(8,128)S(1)} %copy-done), custom_call_target="tpu_custom_call" | custom-call | tf_op jit(solution)/shard_map/pallas_call | solution.py:444
  70.0 1.9 %shard_map.68 = (f32[864,640]{1,0:T(8,128)}, f32[640,256]{1,0:T(8,128)}, f32[864,256]{1,0:T(8,128)}) custom-call(f32[864,640]{1,0:T(8,128)S(1)} %get-tuple-element.10.new, f32[640,256]{1,0:T(8,128)S(1)} %get-tuple-element.11.left, f32[864,256]{1,0:T(8,128)S(1)} %get-tuple-element.12.right, f32[1,256]{1,0:T(1,128)S(1)} %get-tuple-element.13.inv), custom_call_target="tpu_custom_call" | custom-call | tf_op jit(solution)/shard_map/pallas_call | solution.py:491
Async XLA Ops:
  0.6 1.2 %copy-start = (f32[864,256]{1,0:T(8,128)S(1)}, f32[864,256]{1,0:T(8,128)}, u32[]{:S(2)}) copy-start(f32[864,256]{1,0:T(8,128)} %basis_hbm.1) | copy-start | bytes 2654212
